TPU v7x, 256 devices: a whole 4x4x8 slice. The times are simulated.
256 devices in a mesh: role: 2 (over z_hi), dp: 32 (over x, z_lo, core), mp: 4 (over y).
Axes of the slice: x: 4, y: 4, z: 8 (z_hi: 2, z_lo: 4; z = z_hi * 4 + z_lo), core: 2. Of those that a mesh axis runs over, the one named last changes fastest.
Arguments:
- state: float32 [2, 2, 8, 2048, 512], P('role', None, None, 'dp', 'mp'), may hold values from 0 to 1
- embed: bfloat16 [2, 1024, 4096], P('role', 'dp', 'mp'), may hold values from -0.09375 to 0.09375
- mlp: bfloat16 [2, 2, 1024, 4096], P('role', None, 'dp', 'mp'), may hold values from -0.1875 to 0.1875
- mom_embed: float32 [2, 1024, 4096], P('role', 'dp', 'mp'), may hold values from -6 to 6
- mom_mlp: float32 [2, 2, 1024, 4096], P('role', None, 'dp', 'mp'), may hold values from -6 to 6
Outputs:
- state_out: float32 [2, 8, 2048, 512], P(None, None, 'dp', 'mp')
- embed_out: bfloat16 [2, 1024, 4096], P('role', 'dp', 'mp')
- mlp_out: bfloat16 [2, 2, 1024, 4096], P('role', None, 'dp', 'mp')
- mom_embed_out: float32 [2, 1024, 4096], P('role', 'dp', 'mp')
- mom_mlp_out: float32 [2, 2, 1024, 4096], P('role', None, 'dp', 'mp')
All inputs are finite; a program needn't handle non-finite values.
Results may differ from a plain program's by a relative error of at most 0.0034.
Values may be sent and summed in bfloat16 or wider, within the bound.
A program may use at most 128 MiB of HBM per device.

v0:
```python
import jax
import jax.numpy as jnp
from jax import lax
from jax.sharding import PartitionSpec as P

PATCH = 16
STEPS = 4


SUBSTRATE_DIFFUSION = 0.2
CATALYST_DIFFUSION = 0.1
FEED_RATE = 0.037
KILL_RATE = 0.06
TIME_STEP = 0.8
GELU_FACTOR = 0.7978845608028654
MOMENTUM_DECAY = 0.9
LEARNING_RATE = 0.003


def extended(cells, sides, width):
    for axis, dim in sides:
        count = lax.axis_size(axis)
        head = lax.slice_in_dim(cells, 0, width, axis=dim)
        tail = lax.slice_in_dim(cells, cells.shape[dim] - width, cells.shape[dim], axis=dim)
        cells = jnp.concatenate(
            [
                lax.ppermute(tail, axis, [(i, (i + 1) % count) for i in range(count)]),
                cells,
                lax.ppermute(head, axis, [((i + 1) % count, i) for i in range(count)]),
            ],
            axis=dim,
        )
    return cells


def from_behind(value, axis, steps):
    count = lax.axis_size(axis)
    leading, last = (max(0, -steps), min(count, count - steps))
    return lax.ppermute(value, axis, [(source, source + steps) for source in range(leading, last)])


def in_blocks(x, dim, count):
    before, after = (x.shape[:dim], x.shape[dim + 1 :])
    return jnp.moveaxis(x.reshape(*before, count, -1, *after), dim, 0)


def summed_on_arrival(x, axis, dim):
    count = lax.axis_size(axis)
    tiles = lax.all_to_all(in_blocks(x, dim, count), axis, 0, 0, tiled=True)
    return jnp.sum(tiles, axis=0)


def joined_along(tiles, dim):
    tiles = jnp.moveaxis(tiles, 0, dim)
    shape = tiles.shape
    return tiles.reshape(*shape[:dim], shape[dim] * shape[dim + 1], *shape[dim + 2 :])


def copy_for_each(x, axis):
    copies = jnp.broadcast_to(x, (lax.axis_size(axis), *x.shape))
    return lax.all_to_all(copies, axis, split_axis=0, concat_axis=0, tiled=True)


def gathered_copies(x, axis, dim):
    return joined_along(copy_for_each(x, axis), dim)


def react(padded):
    center = padded[:, :, 1:-1, 1:-1]
    below_plane = jnp.concatenate([center[:, :1], center[:, :-1]], axis=1)
    above_plane = jnp.concatenate([center[:, 1:], center[:, -1:]], axis=1)
    beside = below_plane + above_plane + padded[:, :, :-2, 1:-1] + padded[:, :, 2:, 1:-1]
    beside = beside + padded[:, :, 1:-1, :-2] + padded[:, :, 1:-1, 2:]
    laplace = beside - 6.0 * center
    substrate = center[0]
    catalyst = center[1]
    growth = substrate * catalyst * catalyst
    new_substrate = substrate + TIME_STEP * (
        SUBSTRATE_DIFFUSION * laplace[0] - growth + FEED_RATE * (1.0 - substrate)
    )
    new_catalyst = catalyst + TIME_STEP * (
        CATALYST_DIFFUSION * laplace[1] + growth - (FEED_RATE + KILL_RATE) * catalyst
    )
    return jnp.stack([new_substrate, new_catalyst])


def gelu_slope(preact):
    cubic = 0.044715 * preact * preact * preact
    tangent = jnp.tanh(GELU_FACTOR * (preact + cubic))
    return 0.5 * (1.0 + tangent) + 0.5 * preact * (1.0 - tangent * tangent) * GELU_FACTOR * (
        1.0 + 3.0 * 0.044715 * preact * preact
    )


def to_patches(brick):
    extent = brick.shape
    blocks = brick.reshape(
        extent[0], extent[1], extent[2] // PATCH, PATCH, extent[3] // PATCH, PATCH
    )
    blocks = blocks.transpose(2, 4, 0, 1, 3, 5)
    return blocks.reshape(
        extent[2] // PATCH * (extent[3] // PATCH), extent[0] * extent[1] * PATCH * PATCH
    )


def advance(cells):
    padded = extended(cells, (("dp", 2), ("mp", 3)), STEPS)
    for iteration in range(STEPS):
        padded = react(padded)
    return padded


def shards(state, embed, mlp, mom_embed, mom_mlp):
    group_index = lax.axis_index("role")
    start_cells = state[0]
    start_half = start_cells.astype(jnp.bfloat16)
    arranged = lax.all_to_all(to_patches(start_half), "mp", split_axis=1, concat_axis=0, tiled=True)
    initial_rows = from_behind(arranged, "role", 1)
    stacked = jnp.concatenate([embed[0], mlp[0, 0], mlp[0, 1]], axis=1)
    whole = lax.all_gather(stacked, "dp", axis=0, tiled=True)
    cells = advance(start_cells)
    arrived = from_behind(cells, "role", 1)
    state_out = jnp.where(group_index == 0, cells, arrived)
    final_rows = to_patches(arrived.astype(jnp.bfloat16))
    targets = lax.all_to_all(final_rows, "mp", split_axis=1, concat_axis=0, tiled=True)
    feature_cols = embed.shape[2]
    hidden_cols = mlp.shape[3]
    embed_full = whole[:, :feature_cols]
    up_full = whole[:, feature_cols : feature_cols + hidden_cols]
    down_full = whole[:, feature_cols + hidden_cols :]
    patch_rows = initial_rows.shape[0]
    loss_scale = float(patch_rows * lax.axis_size("dp")) ** (-0.5)
    embedded = summed_on_arrival(
        jnp.dot(initial_rows, embed_full.T, preferred_element_type=jnp.float32), "mp", 0
    )
    recip = lax.rsqrt(jnp.mean(embedded * embedded, axis=1, keepdims=True) + 1e-06)
    normed = gathered_copies((embedded * recip).astype(jnp.bfloat16), "mp", 0)
    hidden_pre = jnp.dot(normed, up_full, preferred_element_type=jnp.float32)
    active = jax.nn.gelu(hidden_pre, approximate=True).astype(jnp.bfloat16)
    branch = summed_on_arrival(
        jnp.dot(active, down_full.T, preferred_element_type=jnp.float32), "mp", 0
    )
    stream = gathered_copies((embedded + branch).astype(jnp.bfloat16), "mp", 0)
    predicted = initial_rows.astype(jnp.float32) + jnp.dot(
        stream, embed_full, preferred_element_type=jnp.float32
    )
    residual_grad = ((predicted - targets.astype(jnp.float32)) * loss_scale).astype(jnp.bfloat16)
    stream_grad = summed_on_arrival(
        jnp.dot(residual_grad, embed_full.T, preferred_element_type=jnp.float32), "mp", 0
    )
    stream_sent = gathered_copies(stream_grad.astype(jnp.bfloat16), "mp", 0)
    hidden_grad = (
        jnp.dot(stream_sent, down_full, preferred_element_type=jnp.float32) * gelu_slope(hidden_pre)
    ).astype(jnp.bfloat16)
    normed_grad = summed_on_arrival(
        jnp.dot(hidden_grad, up_full.T, preferred_element_type=jnp.float32), "mp", 0
    )
    embed_grad = (
        stream_grad
        + recip * normed_grad
        - embedded
        * (recip * recip * recip)
        * jnp.mean(normed_grad * embedded, axis=1, keepdims=True)
    )
    embed_sent = gathered_copies(embed_grad.astype(jnp.bfloat16), "mp", 0)
    up_part = jnp.dot(normed.T, hidden_grad, preferred_element_type=jnp.float32)
    down_part = jnp.dot(stream_sent.T, active, preferred_element_type=jnp.float32)
    first = jnp.dot(stream.T, residual_grad, preferred_element_type=jnp.float32)
    grads = lax.psum_scatter(
        jnp.concatenate(
            [
                first + jnp.dot(embed_sent.T, initial_rows, preferred_element_type=jnp.float32),
                up_part,
                down_part,
            ],
            axis=1,
        ),
        "dp",
        scatter_dimension=0,
        tiled=True,
    )
    mirrored = from_behind(grads, "role", -1)
    grads = jnp.where(group_index == 0, mirrored, grads)
    grad_embed_rows = grads[:, :feature_cols]
    grad_mlp_rows = jnp.stack(
        [
            grads[:, feature_cols : feature_cols + hidden_cols],
            grads[:, feature_cols + hidden_cols :],
        ]
    )
    mom_embed_out = MOMENTUM_DECAY * mom_embed + grad_embed_rows[None]
    mom_mlp_out = MOMENTUM_DECAY * mom_mlp + grad_mlp_rows[None]
    embed_out = (embed.astype(jnp.float32) - LEARNING_RATE * mom_embed_out).astype(jnp.bfloat16)
    mlp_out = (mlp.astype(jnp.float32) - LEARNING_RATE * mom_mlp_out).astype(jnp.bfloat16)
    return (state_out, embed_out, mlp_out, mom_embed_out, mom_mlp_out)


def solution(mesh):
    placed = (
        P("role", None, None, "dp", "mp"),
        P("role", "dp", "mp"),
        P("role", None, "dp", "mp"),
        P("role", "dp", "mp"),
        P("role", None, "dp", "mp"),
    )
    return jax.shard_map(
        shards,
        mesh=mesh,
        in_specs=placed,
        out_specs=(
            P(None, None, "dp", "mp"),
            P("role", "dp", "mp"),
            P("role", None, "dp", "mp"),
            P("role", "dp", "mp"),
            P("role", None, "dp", "mp"),
        ),
        check_vma=False,
    )
```

profile of v0, /device:TPU:8, one launch (start us, length us, event | category | flops | bytes accessed | tf_op | source)
XLA Modules:
  0.0 440.3 jit_solution(15371048117641775478)
XLA Ops:
  10.1 6.3 %collective-permute-start.1 = (f32[2,8,4,128]{3,1,2,0:T(8,128)S(1)}, f32[2,8,4,128]{3,1,2,0:T(8,128)S(1)}, u32[]{:S(2)}, u32[]{:S(2)}) collective-permute-start(f32[2,8,4,128]{3,1,2,0:T(8,128)S(1)} %get-tuple-element.66), channel_id=1, source_target_pairs={{4,0},{8,4},{12,8},{16,12},{20,16},{24,20},{28,24},{32,28},{36,32}... | collective-permute-start | bytes 98312 | tf_op jit(solution)/shard_map/ppermute | solution.py:29
  18.0 5.6 %collective-permute-done = f32[2,8,4,128]{3,1,2,0:T(8,128)S(1)} collective-permute-done((f32[2,8,4,128]{3,1,2,0:T(8,128)S(1)}, f32[2,8,4,128]{3,1,2,0:T(8,128)S(1)}, u32[]{:S(2)}, u32[]{:S(2)}) %collective-permute-start) | collective-permute-done | bytes 32800 | tf_op jit(solution)/shard_map/ppermute | solution.py:27
  29.9 3.8 all_to_all.48
  34.4 5.9 %all-to-all-start = ((bf16[32,4,1024]{2,0,1:T(8,128)(2,1)}), bf16[32,4,1024]{2,0,1:T(8,128)(2,1)}, u32[]{:S(2)}, u32[]{:S(2)}) async-start(bf16[32,4,1024]{2,0,1:T(8,128)(2,1)} %copy.89), calls=%async_computation | async-start | bytes 524288 | tf_op jit(solution)/shard_map/all_to_all | solution.py:117
  49.1 6.5 %collective-permute-start.5 = (bf16[128,1024]{1,0:T(8,128)(2,1)}, bf16[128,1024]{1,0:T(8,128)(2,1)S(1)}, u32[]{:S(2)}, u32[]{:S(2)}) collective-permute-start(bf16[128,1024]{1,0:T(8,128)(2,1)} %bitcast.6), channel_id=1, source_target_pairs={{0,128},{1,129},{2,130},{3,131},{4,132},{5,133},{6,134},{7,135},{8... | collective-permute-start | bytes 786440 | tf_op jit(solution)/shard_map/ppermute | solution.py:39
  60.3 26.3 %all-gather.2.cloned.1.call-done = bf16[1024,3072]{1,0:T(8,128)(2,1)} async-done(((bf16[32,3072]{1,0:T(8,128)(2,1)}), bf16[1024,3072]{1,0:T(8,128)(2,1)}) %all-gather.2.cloned.1.call-update) | async-done | bytes 6291472 | tf_op jit(solution)/shard_map/all_gather | solution.py:120
  89.9 4.6 %all-to-all-start.1 = ((f32[4,32,1024]{2,1,0:T(8,128)}), f32[4,32,1024]{2,1,0:T(8,128)}, u32[]{:S(2)}, u32[]{:S(2)}) async-start(f32[4,32,1024]{2,1,0:T(8,128)} %bitcast.8), calls=%async_computation.1 | async-start | bytes 1048576 | tf_op jit(solution)/shard_map/all_to_all | solution.py:49
  96.1 7.1 %all-to-all-done.1 = f32[4,32,1024]{2,1,0:T(8,128)} async-done(((f32[4,32,1024]{2,1,0:T(8,128)}), f32[4,32,1024]{2,1,0:T(8,128)}, u32[]{:S(2)}, u32[]{:S(2)}) %all-to-all-start.1) | async-done | bytes 524320 | tf_op jit(solution)/shard_map/all_to_all | solution.py:49
  105.2 4.8 %all-to-all-start.2 = ((bf16[4,32,1024]{2,1,0:T(8,128)(2,1)}), bf16[4,32,1024]{2,1,0:T(8,128)(2,1)S(1)}, u32[]{:S(2)}, u32[]{:S(2)}) async-start(bf16[4,32,1024]{2,1,0:T(8,128)(2,1)} %broadcast_in_dim.20), calls=%async_computation.2 | async-start | bytes 524288 | tf_op jit(solution)/shard_map/all_to_all | solution.py:61
  117.3 3.4 fusion.2
  120.7 5.5 %all-to-all-start.3 = ((f32[4,32,1024]{2,1,0:T(8,128)}), f32[4,32,1024]{2,1,0:T(8,128)}, u32[]{:S(2)}, u32[]{:S(2)}) async-start(f32[4,32,1024]{2,1,0:T(8,128)} %bitcast.10), calls=%async_computation.3 | async-start | bytes 1048576 | tf_op jit(solution)/shard_map/all_to_all | solution.py:49
  131.5 3.8 all_to_all.56
  136.1 4.9 %all-to-all-start.5 = ((bf16[32,4,1024]{2,0,1:T(8,128)(2,1)}), bf16[32,4,1024]{2,0,1:T(8,128)(2,1)S(1)}, u32[]{:S(2)}, u32[]{:S(2)}) async-start(bf16[32,4,1024]{2,0,1:T(8,128)(2,1)} %copy.91), calls=%async_computation.5 | async-start | bytes 524288 | tf_op jit(solution)/shard_map/all_to_all | solution.py:125
  142.1 4.1 all-to-all-done.5
  146.3 9.1 %all_to_all.72 = bf16[4,32,1024]{2,1,0:T(8,128)(2,1)S(1)} all-to-all(bf16[4,32,1024]{2,1,0:T(8,128)(2,1)S(1)} %broadcast_in_dim.21), channel_id=1, replica_groups=mesh['role'=2,'dp'=32,'mp'=4] {'mp'}, dimensions={0} | all-to-all | bytes 524288 | tf_op jit(solution)/shard_map/all_to_all | solution.py:61
  160.0 10.6 %all_to_all.73 = f32[4,32,1024]{2,1,0:T(8,128)S(1)} all-to-all(f32[4,32,1024]{2,1,0:T(8,128)S(1)} %bitcast.82), channel_id=1, replica_groups=mesh['role'=2,'dp'=32,'mp'=4] {'mp'}, dimensions={0} | all-to-all | bytes 1048576 | tf_op jit(solution)/shard_map/all_to_all | solution.py:49
  170.7 9.1 %all_to_all.74 = bf16[4,32,1024]{2,1,0:T(8,128)(2,1)S(1)} all-to-all(bf16[4,32,1024]{2,1,0:T(8,128)(2,1)S(1)} %broadcast_in_dim.22), channel_id=1, replica_groups=mesh['role'=2,'dp'=32,'mp'=4] {'mp'}, dimensions={0} | all-to-all | bytes 524288 | tf_op jit(solution)/shard_map/all_to_all | solution.py:61
  185.2 4.9 %all-to-all-start.8 = ((f32[4,32,1024]{2,1,0:T(8,128)}), f32[4,32,1024]{2,1,0:T(8,128)S(1)}, u32[]{:S(2)}, u32[]{:S(2)}) async-start(f32[4,32,1024]{2,1,0:T(8,128)} %bitcast.81), calls=%async_computation.8 | async-start | bytes 1048576 | tf_op jit(solution)/shard_map/all_to_all | solution.py:49
  190.1 3.7 fusion.121
  197.7 4.8 %all-to-all-start.9 = ((bf16[4,32,1024]{2,1,0:T(8,128)(2,1)}), bf16[4,32,1024]{2,1,0:T(8,128)(2,1)S(1)}, u32[]{:S(2)}, u32[]{:S(2)}) async-start(bf16[4,32,1024]{2,1,0:T(8,128)(2,1)} %broadcast_in_dim.23), calls=%async_computation.9 | async-start | bytes 524288 | tf_op jit(solution)/shard_map/all_to_all | solution.py:61
  212.5 5.6 %pad_maximum_fusion = f32[1024,3072]{0,1:T(8,128)} fusion(f32[1024,1024]{0,1:T(8,128)S(1)} %copy-done, f32[1024,1024]{0,1:T(8,128)S(1)} %copy-done.1, f32[1024,1024]{0,1:T(8,128)S(1)} %convolution_add_fusion), kind=kLoop, calls=%fused_computation | loop fusion | flops 6291456 | bytes 25165824 | tf_op jit(solution)/shard_map/concatenate | solution.py:170
  218.2 12.6 %copy.99 = f32[1024,3072]{1,0:T(8,128)} copy(f32[1024,3072]{0,1:T(8,128)} %pad_maximum_fusion) | data formatting | bytes 25165824
  230.8 183.1 %reduce-scatter.4.cloned.1.call-done = f32[32,3072]{1,0:T(8,128)} async-done(((f32[1024,3072]{1,0:T(8,128)}), f32[32,3072]{1,0:T(8,128)}) %reduce-scatter.4.cloned.1.call-update) | async-done | bytes 393232 | tf_op jit(solution)/shard_map/reduce_scatter | solution.py:169
  418.8 9.1 %collective-permute-done.6 = f32[32,3072]{1,0:T(8,128)} collective-permute-done((f32[32,3072]{1,0:T(8,128)}, f32[32,3072]{1,0:T(8,128)}, u32[]{:S(2)}, u32[]{:S(2)}) %collective-permute-start.6) | collective-permute-done | bytes 393248 | tf_op jit(solution)/shard_map/ppermute | solution.py:39
  (133 shorter events, 80.5 us)
Async XLA Ops:
  7.2 79.5 %all-gather.2.cloned.1.call-start = ((), (), s32[]{:S(2)}) async-start(), calls=%async_computation.11 | async-start | bytes 6488064 | tf_op jit(solution)/shard_map/all_gather | solution.py:120
  10.1 7.9 %collective-permute-start.1 = (f32[2,8,4,128]{3,1,2,0:T(8,128)S(1)}, f32[2,8,4,128]{3,1,2,0:T(8,128)S(1)}, u32[]{:S(2)}, u32[]{:S(2)}) collective-permute-start(f32[2,8,4,128]{3,1,2,0:T(8,128)S(1)} %get-tuple-element.66), channel_id=1, source_target_pairs={{4,0},{8,4},{12,8},{16,12},{20,16},{24,20},{28,24},{32,28},{36,32}... | collective-permute-start | bytes 98312 | tf_op jit(solution)/shard_map/ppermute | solution.py:29
  16.4 7.2 %collective-permute-start = (f32[2,8,4,128]{3,1,2,0:T(8,128)S(1)}, f32[2,8,4,128]{3,1,2,0:T(8,128)S(1)}, u32[]{:S(2)}, u32[]{:S(2)}) collective-permute-start(f32[2,8,4,128]{3,1,2,0:T(8,128)S(1)} %get-tuple-element.65), channel_id=1, source_target_pairs={{0,4},{4,8},{8,12},{12,16},{16,20},{20,24},{24,28},{28,32},{32,36}... | collective-permute-start | bytes 98312 | tf_op jit(solution)/shard_map/ppermute | solution.py:27
  24.2 16.2 %collective-permute-start.3 = (f32[2,8,72,4]{2,1,3,0:T(8,128)S(1)}, f32[2,8,72,4]{2,1,3,0:T(8,128)S(1)}, u32[]{:S(2)}, u32[]{:S(2)}) collective-permute-start(f32[2,8,72,4]{2,1,3,0:T(8,128)S(1)} %copy.81), channel_id=1, source_target_pairs={{1,0},{2,1},{3,2},{0,3},{5,4},{6,5},{7,6},{4,7},{9,8},{10,9},{11,1... | collective-permute-start | bytes 55304 | tf_op jit(solution)/shard_map/ppermute | solution.py:29
  24.9 15.8 %collective-permute-start.2 = (f32[2,8,72,4]{2,1,3,0:T(8,128)S(1)}, f32[2,8,72,4]{2,1,3,0:T(8,128)S(1)}, u32[]{:S(2)}, u32[]{:S(2)}) collective-permute-start(f32[2,8,72,4]{2,1,3,0:T(8,128)S(1)} %copy.80), channel_id=1, source_target_pairs={{0,1},{1,2},{2,3},{3,0},{4,5},{5,6},{6,7},{7,4},{8,9},{9,10},{10,1... | collective-permute-start | bytes 55304 | tf_op jit(solution)/shard_map/ppermute | solution.py:27
  34.4 14.7 %all-to-all-start = ((bf16[32,4,1024]{2,0,1:T(8,128)(2,1)}), bf16[32,4,1024]{2,0,1:T(8,128)(2,1)}, u32[]{:S(2)}, u32[]{:S(2)}) async-start(bf16[32,4,1024]{2,0,1:T(8,128)(2,1)} %copy.89), calls=%async_computation | async-start | bytes 524288 | tf_op jit(solution)/shard_map/all_to_all | solution.py:117
  49.1 7.2 %copy-start.2 = (f32[2,7,66,130]{3,1,2,0:T(8,128)S(1)}, f32[2,7,66,130]{3,1,2,0:T(8,128)}, u32[]{:S(2)}) copy-start(f32[2,7,66,130]{3,1,2,0:T(8,128)} %get-tuple-element.58) | copy-start | bytes 1441444
  49.1 11.2 %collective-permute-start.5 = (bf16[128,1024]{1,0:T(8,128)(2,1)}, bf16[128,1024]{1,0:T(8,128)(2,1)S(1)}, u32[]{:S(2)}, u32[]{:S(2)}) collective-permute-start(bf16[128,1024]{1,0:T(8,128)(2,1)} %bitcast.6), channel_id=1, source_target_pairs={{0,128},{1,129},{2,130},{3,131},{4,132},{5,133},{6,134},{7,135},{8... | collective-permute-start | bytes 786440 | tf_op jit(solution)/shard_map/ppermute | solution.py:39
  60.3 29.5 %copy-start.12 = (bf16[128,1024]{1,0:T(8,128)(2,1)}, bf16[128,1024]{1,0:T(8,128)(2,1)S(1)}, u32[]{:S(2)}) copy-start(bf16[128,1024]{1,0:T(8,128)(2,1)S(1)} %collective-permute-done.5) | copy-start | bytes 786436
  89.9 13.3 %all-to-all-start.1 = ((f32[4,32,1024]{2,1,0:T(8,128)}), f32[4,32,1024]{2,1,0:T(8,128)}, u32[]{:S(2)}, u32[]{:S(2)}) async-start(f32[4,32,1024]{2,1,0:T(8,128)} %bitcast.8), calls=%async_computation.1 | async-start | bytes 1048576 | tf_op jit(solution)/shard_map/all_to_all | solution.py:49
  105.2 10.0 %all-to-all-start.2 = ((bf16[4,32,1024]{2,1,0:T(8,128)(2,1)}), bf16[4,32,1024]{2,1,0:T(8,128)(2,1)S(1)}, u32[]{:S(2)}, u32[]{:S(2)}) async-start(bf16[4,32,1024]{2,1,0:T(8,128)(2,1)} %broadcast_in_dim.20), calls=%async_computation.2 | async-start | bytes 524288 | tf_op jit(solution)/shard_map/all_to_all | solution.py:61
  110.3 16.0 %collective-permute-start.4 = (f32[2,8,64,128]{3,2,1,0:T(8,128)S(1)}, f32[2,8,64,128]{3,2,1,0:T(8,128)S(1)}, u32[]{:S(2)}, u32[]{:S(2)}) collective-permute-start(f32[2,8,64,128]{3,2,1,0:T(8,128)S(1)} %copy.84), channel_id=1, source_target_pairs={{0,128},{1,129},{2,130},{3,131},{4,132},{5,133},{6,134},{7,135},{8... | collective-permute-start | bytes 1572872 | tf_op jit(solution)/shard_map/ppermute | solution.py:39
  120.7 15.4 %all-to-all-start.3 = ((f32[4,32,1024]{2,1,0:T(8,128)}), f32[4,32,1024]{2,1,0:T(8,128)}, u32[]{:S(2)}, u32[]{:S(2)}) async-start(f32[4,32,1024]{2,1,0:T(8,128)} %bitcast.10), calls=%async_computation.3 | async-start | bytes 1048576 | tf_op jit(solution)/shard_map/all_to_all | solution.py:49
  136.1 19.3 %copy-start.13 = (bf16[128,1024]{1,0:T(8,128)(2,1)S(1)}, bf16[128,1024]{1,0:T(8,128)(2,1)}, u32[]{:S(2)}) copy-start(bf16[128,1024]{1,0:T(8,128)(2,1)} %copy-done.12) | copy-start | bytes 786436
  136.1 10.2 %all-to-all-start.5 = ((bf16[32,4,1024]{2,0,1:T(8,128)(2,1)}), bf16[32,4,1024]{2,0,1:T(8,128)(2,1)S(1)}, u32[]{:S(2)}, u32[]{:S(2)}) async-start(bf16[32,4,1024]{2,0,1:T(8,128)(2,1)} %copy.91), calls=%async_computation.5 | async-start | bytes 524288 | tf_op jit(solution)/shard_map/all_to_all | solution.py:125
  160.0 19.8 %copy-start.9 = (f32[128,1024]{1,0:T(8,128)S(1)}, f32[128,1024]{1,0:T(8,128)}, u32[]{:S(2)}) copy-start(f32[128,1024]{1,0:T(8,128)} %copy-done.8) | copy-start | bytes 1572868
  185.2 11.5 %all-to-all-start.8 = ((f32[4,32,1024]{2,1,0:T(8,128)}), f32[4,32,1024]{2,1,0:T(8,128)S(1)}, u32[]{:S(2)}, u32[]{:S(2)}) async-start(f32[4,32,1024]{2,1,0:T(8,128)} %bitcast.81), calls=%async_computation.8 | async-start | bytes 1048576 | tf_op jit(solution)/shard_map/all_to_all | solution.py:49
  196.6 6.0 %copy-start.6 = (bf16[4,32,1024]{2,1,0:T(8,128)(2,1)S(1)}, bf16[4,32,1024]{2,1,0:T(8,128)(2,1)}, u32[]{:S(2)}) copy-start(bf16[4,32,1024]{2,1,0:T(8,128)(2,1)} %copy-done.5) | copy-start | bytes 786436
  197.7 10.1 %all-to-all-start.9 = ((bf16[4,32,1024]{2,1,0:T(8,128)(2,1)}), bf16[4,32,1024]{2,1,0:T(8,128)(2,1)S(1)}, u32[]{:S(2)}, u32[]{:S(2)}) async-start(bf16[4,32,1024]{2,1,0:T(8,128)(2,1)} %broadcast_in_dim.23), calls=%async_computation.9 | async-start | bytes 524288 | tf_op jit(solution)/shard_map/all_to_all | solution.py:61
  202.6 5.2 %copy-start.14 = (bf16[128,1024]{1,0:T(8,128)(2,1)S(1)}, bf16[128,1024]{1,0:T(8,128)(2,1)}, u32[]{:S(2)}) copy-start(bf16[128,1024]{1,0:T(8,128)(2,1)} %copy-done.12) | copy-start | bytes 786436
  202.6 211.4 %reduce-scatter.4.cloned.1.call-start = ((), (), s32[]{:S(2)}) async-start(), calls=%async_computation.12 | async-start | bytes 12976128 | tf_op jit(solution)/shard_map/reduce_scatter | solution.py:169
  230.8 184.4 %copy-start.16 = (bf16[1,32,1024]{2,1,0:T(8,128)(2,1)S(1)}, bf16[1,32,1024]{2,1,0:T(8,128)(2,1)}, u32[]{:S(2)}) copy-start(bf16[1,32,1024]{2,1,0:T(8,128)(2,1)} %param.6) | copy-start | bytes 196612
  230.8 185.3 %copy-start.18 = (f32[1,32,1024]{2,1,0:T(8,128)S(1)}, f32[1,32,1024]{2,1,0:T(8,128)}, u32[]{:S(2)}) copy-start(f32[1,32,1024]{2,1,0:T(8,128)} %param.8) | copy-start | bytes 393220
  413.9 13.9 %collective-permute-start.6 = (f32[32,3072]{1,0:T(8,128)}, f32[32,3072]{1,0:T(8,128)}, u32[]{:S(2)}, u32[]{:S(2)}) collective-permute-start(f32[32,3072]{1,0:T(8,128)} %reduce-scatter.4.cloned.1.call-done), channel_id=1, source_target_pairs={{128,0},{129,1},{130,2},{131,3},{132,4},{133,5},{134,6},{135,7},{1... | collective-permute-start | bytes 1179656 | tf_op jit(solution)/shard_map/ppermute | solution.py:39
  (11 other events, 26.1 us)
Sparse Core Ops, SparseCore 0:
  10.4 76.1 all-gather.1
  231.0 182.9 reduce-scatter.3
where the time goes:
time: 442 us; the launch traced here: 440 us
  waiting for transfers between devices  244 us (55%)
  starting transfers between devices  54.6 us (12%)
  local copies, waits for them, and re-layouts  44.4 us (10%)
  matrix products  31.1 us (7%)
  blocking collectives  28.7 us (6%)
  other arithmetic  22.5 us (5%)
  between operations  14.5 us (3%)
    reduce_scatter x1, waiting for transfers between devices, shards(): lax.psum_scatter(jnp.concatenate([first + jnp.dot(embed_sent.T, initial_r...  183 us
    all_gather x1, waiting for transfers between devices, shards(): whole = lax.all_gather(stacked, 'dp', axis=0, tiled=True)  26.3 us
    unnamed x46, local copies, waits for them, and re-layouts  20.4 us
    all_to_all x2, blocking collectives, copy_for_each(): return lax.all_to_all(copies, axis, split_axis=0, concat_axis=0, tiled=True)  18.1 us
    all_to_all x3, starting transfers between devices, summed_on_arrival(): tiles = lax.all_to_all(in_blocks(x, dim, count), axis, 0, 0, tiled=True)  15.1 us
    ppermute x3, waiting for transfers between devices, from_behind(): lax.ppermute(value, axis, [(source, source + steps) for source in range(l...  11.9 us
    ppermute x3, starting transfers between devices, from_behind(): lax.ppermute(value, axis, [(source, source + steps) for source in range(l...  10.6 us
    all_to_all x1, blocking collectives, summed_on_arrival(): tiles = lax.all_to_all(in_blocks(x, dim, count), axis, 0, 0, tiled=True)  10.6 us
  transfers between devices with their start and end apart: 16, of which 11 were waited for; matrix products, arithmetic and copies ran while one was open for 10% of the time, Pallas kernels for 0%

commit v1 on v0

v1 whole, which is shorter than its diff:
```python
import jax
import jax.numpy as jnp
from jax import lax
from jax.experimental import pallas as pl
from jax.experimental.pallas import tpu as pltpu
from jax.sharding import PartitionSpec as P

PATCH = 16
STEPS = 4


SUBSTRATE_DIFFUSION = 0.2
CATALYST_DIFFUSION = 0.1
FEED_RATE = 0.037
KILL_RATE = 0.06
TIME_STEP = 0.8
GELU_FACTOR = 0.7978845608028654
MOMENTUM_DECAY = 0.9
LEARNING_RATE = 0.003

BF16 = jnp.bfloat16
F32 = jnp.float32
MESH = pl.DeviceIdType.MESH
ROWS = 128
OWN = 32
D = 1024
COLS = 1024
E, U, W = 0, 1, 2


def extended(cells, sides, width):
    for axis, dim in sides:
        count = lax.axis_size(axis)
        head = lax.slice_in_dim(cells, 0, width, axis=dim)
        tail = lax.slice_in_dim(cells, cells.shape[dim] - width, cells.shape[dim], axis=dim)
        cells = jnp.concatenate(
            [
                lax.ppermute(tail, axis, [(i, (i + 1) % count) for i in range(count)]),
                cells,
                lax.ppermute(head, axis, [((i + 1) % count, i) for i in range(count)]),
            ],
            axis=dim,
        )
    return cells


def react(padded):
    center = padded[:, :, 1:-1, 1:-1]
    below_plane = jnp.concatenate([center[:, :1], center[:, :-1]], axis=1)
    above_plane = jnp.concatenate([center[:, 1:], center[:, -1:]], axis=1)
    beside = below_plane + above_plane + padded[:, :, :-2, 1:-1] + padded[:, :, 2:, 1:-1]
    beside = beside + padded[:, :, 1:-1, :-2] + padded[:, :, 1:-1, 2:]
    laplace = beside - 6.0 * center
    substrate = center[0]
    catalyst = center[1]
    growth = substrate * catalyst * catalyst
    new_substrate = substrate + TIME_STEP * (
        SUBSTRATE_DIFFUSION * laplace[0] - growth + FEED_RATE * (1.0 - substrate)
    )
    new_catalyst = catalyst + TIME_STEP * (
        CATALYST_DIFFUSION * laplace[1] + growth - (FEED_RATE + KILL_RATE) * catalyst
    )
    return jnp.stack([new_substrate, new_catalyst])


def to_blocks(brick):
    extent = brick.shape
    parts = brick.reshape(
        extent[0], 2, extent[1] // 2, extent[2] // PATCH, PATCH, extent[3] // PATCH, PATCH
    )
    parts = parts.transpose(0, 1, 3, 5, 2, 4, 6)
    return parts.reshape(4, OWN, COLS)


def advance(cells):
    padded = extended(cells, (("dp", 2), ("mp", 3)), STEPS)
    for iteration in range(STEPS):
        padded = react(padded)
    return padded


def kernel(
    xs, ts, w, out,
    wf, px, yd, tg, part, sbuf, rbuf, nf, dyf, act, slope, dhid, ered, dyred,
    acc, cs, cr, xs1, xr1, xs2, xr2, vsum, zs1, zr1, zs2, zr2,
    role_s, role_r, x_s, x_r, ag_s, ag_r, rs_s, rs_r, mg_s, mg_r, gr_s, gr_r,
):
    role = lax.axis_index("role")
    dp = lax.axis_index("dp")
    mp = lax.axis_index("mp")
    x, z, c = dp // 8, (dp // 2) % 4, dp % 2

    def dev(x_, z_, c_):
        return {"dp": (x_ * 4 + z_) * 2 + c_}

    x1, x2, x3 = x + 1 - 2 * (x % 2), (x + 2) % 4, 3 - x
    z1, z2 = z + 1 - 2 * (z % 2), (z + 2) % 4
    z3 = (z1 + 2) % 4
    c1 = 1 - c
    to_c, to_x1, to_x3 = dev(x, z, c1), dev(x1, z, c), dev(x3, z, c)
    to_z1, to_z2 = dev(x, z1, c), dev(x, z2, c)
    other = [(mp + o) % 4 for o in range(4)]

    def at(start, size):
        return pl.ds(pl.multiple_of(start, 32), size)

    barrier = pltpu.get_barrier_semaphore()
    friends = [to_c, to_x1, to_x3, to_z1, to_z2]
    friends += [{"mp": other[o]} for o in (1, 2, 3)]
    friends += [{"role": 1 - role, "mp": other[o]} for o in range(4)]
    for friend in friends:
        pl.semaphore_signal(barrier, inc=1, device_id=friend, device_id_type=MESH)
    pl.semaphore_wait(barrier, len(friends))

    started = []

    def copy(src, dst, ssem, rsem, to):
        return pltpu.make_async_remote_copy(
            src_ref=src, dst_ref=dst, send_sem=ssem, recv_sem=rsem, device_id=to, device_id_type=MESH
        )

    def send(src, dst, ssem, rsem, to):
        made = copy(src, dst, ssem, rsem, to)
        made.start()
        started.append(made)

    def arrive(dst, ssem, rsem, frm):
        copy(dst, dst, ssem, rsem, frm).wait_recv()

    own_rows = at(c * 512 + x * 128 + z * 32, 32)

    def weights_across(k):
        return copy(w.at[k], wf.at[k, own_rows], role_s.at[k], role_r.at[k], {"role": 0})

    def weights_here(k):
        return pltpu.make_async_copy(w.at[k], wf.at[k, own_rows], role_r.at[k])

    def patches(which, src, dst, base):
        made = []
        for o in range(4):
            rows = at(base + 32 * mp, 32)
            for r in (1, 0):
                if o == 0 and r == 0:
                    continue
                made.append(
                    copy(src.at[other[o]], dst.at[rows], x_s.at[which, r, o], x_r.at[which, o],
                         {"role": r, "mp": other[o]})
                )
        return made

    def patches_here(which, src, dst, base):
        return pltpu.make_async_copy(src.at[mp], dst.at[at(base + 32 * mp, 32)], x_r.at[which, 0])

    @pl.when(role == 1)
    def _():
        for k in (E, U, W):
            weights_across(k).start()
            weights_here(k).start()

    @pl.when(role == 0)
    def _():
        for made in patches(0, xs, px, 128):
            made.start()
        patches_here(0, xs, px, 128).start()
        for made in patches(1, ts, tg, 0):
            made.start()
        patches_here(1, ts, tg, 0).start()

    def patches_arrive(which, dst, base):
        for o in range(4):
            frm = (mp + 4 - o) % 4
            arrive(dst.at[at(base + 32 * frm, 32)], x_s.at[which, 1, o], x_r.at[which, o], {"mp": other[1]})

    def block(x_, z_=0, c_=c):
        return c_ * 512 + x_ * 128 + z_ * 32

    def g_send(k, i, start, size, to):
        rows = at(start, size)
        send(wf.at[k, rows], wf.at[k, rows], ag_s.at[k, i], ag_r.at[k, i], to)

    def g_arrive(k, i, start, size, frm):
        arrive(wf.at[k, at(start, size)], ag_s.at[k, i], ag_r.at[k, i], frm)

    def gather0(k):
        arrive(wf.at[k, own_rows], role_s.at[k], role_r.at[k], {"role": 1 - role})
        g_send(k, 0, block(x, z), 32, to_z2)
        g_send(k, 1, block(x, z), 32, to_z1)

    def gather1(k):
        g_arrive(k, 0, block(x, z2), 32, to_z2)
        g_send(k, 2, block(x, z2), 32, to_z1)

    def gather2(k):
        g_arrive(k, 1, block(x, z1), 32, to_z1)
        g_arrive(k, 2, block(x, z3), 32, to_z1)
        g_send(k, 3, block(x), 128, to_x1)
        g_send(k, 4, block(x), 128, to_x3)
        g_send(k, 7, block(x), 128, to_c)

    def gather3(k):
        g_arrive(k, 3, block(x1), 128, to_x1)
        g_send(k, 5, block(x1), 64, to_x3)
        g_send(k, 8, block(x1), 128, to_c)
        g_arrive(k, 4, block(x3), 128, to_x3)
        g_send(k, 6, block(x3) + 64, 64, to_x1)
        g_send(k, 9, block(x3), 128, to_c)

    def gather4(k):
        g_arrive(k, 5, block(x2), 64, to_x3)
        g_send(k, 10, block(x2), 64, to_c)
        g_arrive(k, 6, block(x2) + 64, 64, to_x1)
        g_send(k, 11, block(x2) + 64, 64, to_c)

    def gather5(k):
        g_arrive(k, 7, block(x, 0, c1), 128, to_c)
        g_arrive(k, 8, block(x1, 0, c1), 128, to_c)
        g_arrive(k, 9, block(x3, 0, c1), 128, to_c)
        g_arrive(k, 10, block(x2, 0, c1), 64, to_c)
        g_arrive(k, 11, block(x2, 0, c1) + 64, 64, to_c)

    def tiles(width, body):
        @pl.loop(0, COLS // width)
        def _(t):
            body(pl.ds(pl.multiple_of(t * width, width), width))

    def with_rows(lhs, k, rows):
        return lax.dot_general(lhs, wf[k, rows, :], (((1,), (1,)), ((), ())), preferred_element_type=F32)

    def with_cols(lhs, k, cols):
        return jnp.dot(lhs, wf[k, :, cols], preferred_element_type=F32)

    mine = at(32 * mp, 32)

    def partial_sums(i, lhs, k):
        def body(cols):
            value = with_rows(lhs[...], k, cols)
            part[:, cols] = value
            sbuf[i, :, cols] = value.astype(BF16)

        tiles(256, body)
        for o in (2, 1, 3):
            send(sbuf.at[i, at(32 * other[o], 32)], rbuf.at[i, o - 1], rs_s.at[i, o - 1], rs_r.at[i, o - 1],
                 {"mp": other[o]})

    def summed(i):
        total = part[mine, :]
        for o in (1, 3, 2):
            arrive(rbuf.at[i, o - 1], rs_s.at[i, o - 1], rs_r.at[i, o - 1], {"mp": other[o]})
            total = total + rbuf[i, o - 1].astype(F32)
        return total

    def spread(i, dst, base, value):
        rows = at(base + 32 * mp, 32)
        dst[rows, :] = value
        for o in (2, 1, 3):
            send(dst.at[rows], dst.at[rows], mg_s.at[i, o - 1], mg_r.at[i, o - 1], {"mp": other[o]})

    def spread_arrive(i, dst, base):
        for o in (1, 3, 2):
            rows = at(base + 32 * ((mp + 4 - o) % 4), 32)
            arrive(dst.at[rows], mg_s.at[i, o - 1], mg_r.at[i, o - 1], {"mp": other[o]})

    def terms(k, lhs, rhs):
        def product(rows, cols):
            return lax.dot_general(lhs[:, rows], rhs[:, cols], (((0,), (0,)), ((), ())), preferred_element_type=F32)

        @pl.loop(0, 2)
        def _(t):
            rows = pl.ds(pl.multiple_of(c1 * 512 + t * 256, 256), 256)
            for s in (0, 1):
                cols = pl.ds(512 * s, 512)
                cs[k, pl.ds(pl.multiple_of(t * 256, 256), 256), cols] = product(rows, cols).astype(BF16)

        send(cs.at[k], cr.at[k], gr_s.at[k, 0], gr_r.at[k, 0], to_c)

        @pl.loop(0, 2)
        def _(t):
            rows = pl.ds(pl.multiple_of(c * 512 + t * 256, 256), 256)
            for s in (0, 1):
                cols = pl.ds(512 * s, 512)
                acc[k, pl.ds(pl.multiple_of(t * 256, 256), 256), cols] = product(rows, cols)

    def chunks(count, body):
        @pl.loop(0, count)
        def _(t):
            body(pl.multiple_of(t * 32, 32))

    def pair(k, start):
        return acc[k, pl.ds(start, 32), :] + cr[k, pl.ds(start, 32), :].astype(F32)

    def reduce1(k):
        arrive(cr.at[k], gr_s.at[k, 0], gr_r.at[k, 0], to_c)

        def body(t):
            for h, far in ((0, x3), (1, x1)):
                for i, xb in ((0, far), (1, x2)):
                    xs1[k, h, i, pl.ds(t, 32), :] = pair(k, pl.multiple_of(xb * 128 + h * 64 + t, 32)).astype(BF16)

        chunks(2, body)
        send(xs1.at[k, 0], xr1.at[k, 0], gr_s.at[k, 1], gr_r.at[k, 1], to_x3)
        send(xs1.at[k, 1], xr1.at[k, 1], gr_s.at[k, 2], gr_r.at[k, 2], to_x1)

    def reduce2(k):
        arrive(xr1.at[k, 0], gr_s.at[k, 1], gr_r.at[k, 1], to_x3)
        arrive(xr1.at[k, 1], gr_s.at[k, 2], gr_r.at[k, 2], to_x1)

        def body(t):
            for h, near in ((0, x1), (1, x3)):
                value = pair(k, pl.multiple_of(near * 128 + h * 64 + t, 32)) + xr1[k, h, 1, pl.ds(t, 32), :].astype(F32)
                xs2[k, h, pl.ds(t, 32), :] = value.astype(BF16)

        chunks(2, body)
        send(xs2.at[k, 0], xr2.at[k, 0], gr_s.at[k, 3], gr_r.at[k, 3], to_x1)
        send(xs2.at[k, 1], xr2.at[k, 1], gr_s.at[k, 4], gr_r.at[k, 4], to_x3)

    def reduce3(k):
        arrive(xr2.at[k, 0], gr_s.at[k, 3], gr_r.at[k, 3], to_x1)
        arrive(xr2.at[k, 1], gr_s.at[k, 4], gr_r.at[k, 4], to_x3)

        def body(t):
            for h in (0, 1):
                value = pair(k, pl.multiple_of(x * 128 + h * 64 + t, 32))
                value = value + xr1[k, h, 0, pl.ds(t, 32), :].astype(F32) + xr2[k, h, pl.ds(t, 32), :].astype(F32)
                vsum[k, pl.ds(pl.multiple_of(h * 64 + t, 32), 32), :] = value

        chunks(2, body)
        zs1[k, 0] = vsum[k, at(z1 * 32, 32), :].astype(BF16)
        zs1[k, 1] = vsum[k, at(z3 * 32, 32), :].astype(BF16)
        send(zs1.at[k], zr1.at[k], gr_s.at[k, 5], gr_r.at[k, 5], to_z1)

    def reduce4(k):
        arrive(zr1.at[k], gr_s.at[k, 5], gr_r.at[k, 5], to_z1)
        zs2[k] = (vsum[k, at(z2 * 32, 32), :] + zr1[k, 1].astype(F32)).astype(BF16)
        send(zs2.at[k], zr2.at[k], gr_s.at[k, 6], gr_r.at[k, 6], to_z2)

    def reduce5(k):
        arrive(zr2.at[k], gr_s.at[k, 6], gr_r.at[k, 6], to_z2)
        out[k] = vsum[k, at(z * 32, 32), :] + zr1[k, 0].astype(F32) + zr2[k].astype(F32)

    for k in (E, U, W):
        gather0(k)
    gather1(E)
    gather2(E)
    gather1(U)
    gather1(W)
    gather3(E)
    gather2(U)
    gather4(E)
    gather5(E)

    patches_arrive(0, px, 128)
    xin = px.at[128:256]
    partial_sums(0, xin, E)
    gather2(W)
    gather3(U)
    e = summed(0)
    recip = lax.rsqrt(jnp.mean(e * e, axis=1, keepdims=True) + 1e-06)
    ered[...] = e
    spread(0, nf, 0, (e * recip).astype(BF16))
    gather4(U)
    gather3(W)
    gather5(U)
    spread_arrive(0, nf, 0)

    def hidden(cols):
        pre = with_cols(nf[...], U, cols)
        square = pre * pre
        tangent = jnp.tanh(GELU_FACTOR * (pre + 0.044715 * square * pre))
        act[:, cols] = (0.5 * pre * (1.0 + tangent)).astype(BF16)
        slope[:, cols] = 0.5 * (1.0 + tangent) + 0.5 * pre * (1.0 - tangent * tangent) * GELU_FACTOR * (
            1.0 + 3.0 * 0.044715 * square
        )

    tiles(256, hidden)
    gather4(W)
    gather5(W)
    partial_sums(1, act, W)
    spread(1, yd, 0, (ered[...] + summed(1)).astype(BF16))
    patches_arrive(1, tg, 0)
    spread_arrive(1, yd, 0)

    def residual(cols):
        pred = px[128:256, cols].astype(F32) + with_cols(yd[0:128, :], E, cols)
        px[0:128, cols] = ((pred - tg[:, cols].astype(F32)) * (1.0 / 64.0)).astype(BF16)

    tiles(256, residual)
    partial_sums(2, px.at[0:128], E)
    dy = summed(2)
    dyred[...] = dy
    spread(2, dyf, 0, dy.astype(BF16))
    spread_arrive(2, dyf, 0)

    def hidden_back(cols):
        dhid[:, cols] = (with_cols(dyf[...], W, cols) * slope[:, cols]).astype(BF16)

    tiles(256, hidden_back)
    partial_sums(3, dhid, U)
    terms(W, dyf, act)
    dn = summed(3)
    e = ered[...]
    recip = lax.rsqrt(jnp.mean(e * e, axis=1, keepdims=True) + 1e-06)
    de = dyred[...] + recip * dn - e * (recip * recip * recip) * jnp.mean(dn * e, axis=1, keepdims=True)
    spread(3, yd, 128, de.astype(BF16))
    reduce1(W)
    terms(U, nf, dhid)
    spread_arrive(3, yd, 128)
    terms(E, yd, px)
    reduce1(U)
    reduce2(W)
    reduce1(E)
    reduce2(U)
    reduce3(W)
    reduce2(E)
    reduce3(U)
    reduce4(W)
    reduce3(E)
    reduce4(U)
    reduce5(W)
    reduce4(E)
    reduce5(U)
    reduce5(E)

    for made in started:
        made.wait_send()

    @pl.when(role == 1)
    def _():
        for k in (E, U, W):
            weights_across(k).wait_send()

    @pl.when(role == 0)
    def _():
        for made in patches(0, xs, px, 128) + patches(1, ts, tg, 0):
            made.wait_send()


def gradients(xs, ts, w):
    vmem = pl.BlockSpec(memory_space=pltpu.VMEM)
    dma = pltpu.SemaphoreType.DMA
    return pl.pallas_call(
        kernel,
        name="train",
        out_shape=jax.ShapeDtypeStruct((3, OWN, COLS), F32),
        in_specs=[vmem] * 3,
        out_specs=vmem,
        scratch_shapes=[
            pltpu.VMEM((3, D, COLS), BF16),
            pltpu.VMEM((2 * ROWS, COLS), BF16),
            pltpu.VMEM((2 * ROWS, D), BF16),
            pltpu.VMEM((ROWS, COLS), BF16),
            pltpu.VMEM((ROWS, D), F32),
            pltpu.VMEM((4, ROWS, D), BF16),
            pltpu.VMEM((4, 3, OWN, D), BF16),
            pltpu.VMEM((ROWS, D), BF16),
            pltpu.VMEM((ROWS, D), BF16),
            pltpu.VMEM((ROWS, COLS), BF16),
            pltpu.VMEM((ROWS, COLS), F32),
            pltpu.VMEM((ROWS, COLS), BF16),
            pltpu.VMEM((OWN, D), F32),
            pltpu.VMEM((OWN, D), F32),
            pltpu.VMEM((3, 512, COLS), F32),
            pltpu.VMEM((3, 512, COLS), BF16),
            pltpu.VMEM((3, 512, COLS), BF16),
            pltpu.VMEM((3, 2, 2, 64, COLS), BF16),
            pltpu.VMEM((3, 2, 2, 64, COLS), BF16),
            pltpu.VMEM((3, 2, 64, COLS), BF16),
            pltpu.VMEM((3, 2, 64, COLS), BF16),
            pltpu.VMEM((3, 128, COLS), F32),
            pltpu.VMEM((3, 2, OWN, COLS), BF16),
            pltpu.VMEM((3, 2, OWN, COLS), BF16),
            pltpu.VMEM((3, OWN, COLS), BF16),
            pltpu.VMEM((3, OWN, COLS), BF16),
            dma((3,)), dma((3,)),
            dma((2, 2, 4)), dma((2, 4)),
            dma((3, 12)), dma((3, 12)),
            dma((4, 3)), dma((4, 3)),
            dma((4, 3)), dma((4, 3)),
            dma((3, 7)), dma((3, 7)),
        ],
        compiler_params=pltpu.CompilerParams(
            collective_id=0, has_side_effects=True, vmem_limit_bytes=52 * 1024 * 1024
        ),
        cost_estimate=pl.CostEstimate(flops=6 * 10**9, bytes_accessed=4 * 10**8, transcendentals=10**5),
    )(xs, ts, w)


def shards(state, embed, mlp, mom_embed, mom_mlp):
    group_index = lax.axis_index("role")
    start_cells = state[0]
    cells = advance(start_cells)
    arrived = lax.ppermute(cells, "role", [(0, 1)])
    state_out = jnp.where(group_index == 0, cells, arrived)
    grads = gradients(
        to_blocks(start_cells.astype(BF16)),
        to_blocks(cells.astype(BF16)),
        jnp.concatenate([embed, mlp[0]], axis=0),
    )
    mom_embed_out = MOMENTUM_DECAY * mom_embed + grads[:1]
    mom_mlp_out = MOMENTUM_DECAY * mom_mlp + grads[None, 1:]
    embed_out = (embed.astype(F32) - LEARNING_RATE * mom_embed_out).astype(BF16)
    mlp_out = (mlp.astype(F32) - LEARNING_RATE * mom_mlp_out).astype(BF16)
    return (state_out, embed_out, mlp_out, mom_embed_out, mom_mlp_out)


def solution(mesh):
    placed = (
        P("role", None, None, "dp", "mp"),
        P("role", "dp", "mp"),
        P("role", None, "dp", "mp"),
        P("role", "dp", "mp"),
        P("role", None, "dp", "mp"),
    )
    return jax.shard_map(
        shards,
        mesh=mesh,
        in_specs=placed,
        out_specs=(
            P(None, None, "dp", "mp"),
            P("role", "dp", "mp"),
            P("role", None, "dp", "mp"),
            P("role", "dp", "mp"),
            P("role", None, "dp", "mp"),
        ),
        check_vma=False,
    )
```

time: 442 us -> 208 us (0.47)
  waiting for transfers between devices: 244 us -> 1.62 us
  Pallas kernels: 0 us -> 158 us
  starting transfers between devices: 54.6 us -> 17.1 us
  matrix products: 31.1 us -> 0 us
  blocking collectives: 28.7 us -> 0 us
  local copies, waits for them, and re-layouts: 44.4 us -> 18.7 us
  between operations: 14.5 us -> 0.93 us
  other arithmetic: 22.5 us -> 12.1 us
    reduce_scatter x1 -> x0, waiting for transfers between devices: 183 us -> none  [shards(): lax.psum_scatter(jnp.concatenate([first + jnp.dot(embed_sent.T, initial_r...]
    pallas_call x0 -> x1, Pallas kernels: none -> 158 us  [gradients(): pl.pallas_call(kernel, name='train', out_shape=jax.ShapeDtypeStruct((3, O...]
    all_to_all x7 -> x0, starting transfers between devices: 35.5 us -> none  [the longest x3 15.1 us: summed_on_arrival(): tiles = lax.all_to_all(in_blocks(x, dim, count), axis, 0, 0, tiled=True)]
    dot_general x11 -> x0, matrix products: 31.1 us -> none  [the longest x1 3.68 us: shards(): first = jnp.dot(stream.T, residual_grad, preferred_element_type=jnp.float32)]
    all_to_all x3 -> x0, blocking collectives: 28.7 us -> none  [the longest x2 18.1 us: copy_for_each(): return lax.all_to_all(copies, axis, split_axis=0, concat_axis=0, tiled=True)]
    all_gather x1 -> x0, waiting for transfers between devices: 26.3 us -> none  [shards(): whole = lax.all_gather(stacked, 'dp', axis=0, tiled=True)]
    unnamed x46 -> x12, local copies, waits for them, and re-layouts: 20.4 us -> 2.28 us
    all_to_all x7 -> x0, waiting for transfers between devices: 15.8 us -> none  [the longest x3 7.23 us: summed_on_arrival(): tiles = lax.all_to_all(in_blocks(x, dim, count), axis, 0, 0, tiled=True)]
  transfers between devices with their start and end apart: 16 -> 5, of which waited for: 11 -> 1; matrix products, arithmetic and copies ran while one was open for 10% -> 5% of each run, Pallas kernels for 0% -> 76%
where the time goes in v1:
time: 208 us
  Pallas kernels  158 us (76%)
  local copies, waits for them, and re-layouts  18.7 us (9%)
  starting transfers between devices  17.1 us (8%)
  other arithmetic  12.1 us (6%)
    pallas_call x1, Pallas kernels, gradients(): pl.pallas_call(kernel, name='train', out_shape=jax.ShapeDtypeStruct((3, O...  158 us
    ppermute x1, starting transfers between devices, shards(): arrived = lax.ppermute(cells, 'role', [(0, 1)])  8.57 us
    reshape x2, local copies, waits for them, and re-layouts, to_blocks(): return parts.reshape(4, OWN, COLS)  8.45 us
    ppermute x2, starting transfers between devices, extended(): lax.ppermute(head, axis, [((i + 1) % count, i) for i in range(count)])  6.83 us
    sub x4, other arithmetic, react(): laplace = beside - 6.0 * center  4.31 us
  transfers between devices with their start and end apart: 5, of which 1 were waited for; matrix products, arithmetic and copies ran while one was open for 5% of the time, Pallas kernels for 76%

profile of v1, /device:TPU:8, one launch (start us, length us, event | category | flops | bytes accessed | tf_op | source)
XLA Modules:
  0.0 208.2 jit_solution(5750158919628903090)
XLA Ops:
  0.6 1.4 copy.40
  2.1 6.3 %collective-permute-start.1 = (f32[2,8,4,128]{3,1,2,0:T(8,128)S(1)}, f32[2,8,4,128]{3,1,2,0:T(8,128)S(1)}, u32[]{:S(2)}, u32[]{:S(2)}) collective-permute-start(f32[2,8,4,128]{3,1,2,0:T(8,128)S(1)} %get-tuple-element.53), channel_id=1, source_target_pairs={{4,0},{8,4},{12,8},{16,12},{20,16},{24,20},{28,24},{32,28},{36,32}... | collective-permute-start | bytes 98312 | tf_op jit(solution)/shard_map/ppermute | solution.py:40
  8.4 1.6 collective-permute-done
  10.6 1.6 collective-permute-start.2
  13.0 1.4 convert_element_type.23
  14.4 1.9 copy.39
  16.3 4.9 %reshape.24.xs = bf16[4,32,1024]{2,1,0:T(8,128)(2,1)S(1)} reshape(bf16[2,2,4,8,4,16,16]{6,5,4,3,2,1,0:T(8,128)(2,1)} %bitcast.22) | data formatting | bytes 524288 | tf_op jit(solution)/shard_map/reshape | solution.py:72
  22.4 0.7 fusion.79
  23.0 0.7 fusion.80
  23.7 1.3 fusion
  25.4 0.6 fusion.71
  26.0 0.6 fusion.5
  26.7 1.2 fusion.3
  29.0 0.6 fusion.17
  29.6 1.2 fusion.15
  32.7 0.7 stack.30
  33.4 0.7 stack.31
  34.0 0.7 maximum_bitcast_fusion
  35.4 3.6 %reshape.25.ts = bf16[4,32,1024]{2,1,0:T(8,128)(2,1)S(1)} reshape(bf16[2,2,4,8,4,16,16]{6,5,4,3,2,1,0:T(8,128)(2,1)S(1)} %copy.34) | data formatting | bytes 524288 | tf_op jit(solution)/shard_map/reshape | solution.py:72
  39.1 8.6 %collective-permute-start.4 = (f32[2,8,64,128]{3,2,1,0:T(8,128)S(1)}, f32[2,8,64,128]{3,2,1,0:T(8,128)S(1)}, u32[]{:S(2)}, u32[]{:S(2)}) collective-permute-start(f32[2,8,64,128]{3,2,1,0:T(8,128)S(1)} %copy.29), channel_id=1, source_target_pairs={{0,128},{1,129},{2,130},{3,131},{4,132},{5,133},{6,134},{7,135},{8... | collective-permute-start | bytes 1572872 | tf_op jit(solution)/shard_map/ppermute | solution.py:491
  47.7 157.8 %train.1 = f32[3,32,1024]{2,1,0:T(8,128)S(1)} custom-call(bf16[4,32,1024]{2,1,0:T(8,128)(2,1)S(1)} %reshape.24.xs, bf16[4,32,1024]{2,1,0:T(8,128)(2,1)S(1)} %reshape.25.ts, bf16[3,32,1024]{2,1,0:T(8,128)(2,1)S(1)} %pad_maximum_fusion.5.w), custom_call_target="tpu_custom_call" | custom-call | flops 6000000000 | bytes 400000000 | tf_op jit(solution)/shard_map/train/pallas_call | solution.py:440
  205.5 0.7 subtract_convert_fusion.1
  206.2 0.8 subtract_convert_fusion
  207.3 0.9 copy.35
  (40 shorter events, 6.9 us)
Async XLA Ops:
  2.0 8.0 %collective-permute-start = (f32[2,8,4,128]{3,1,2,0:T(8,128)S(1)}, f32[2,8,4,128]{3,1,2,0:T(8,128)S(1)}, u32[]{:S(2)}, u32[]{:S(2)}) collective-permute-start(f32[2,8,4,128]{3,1,2,0:T(8,128)S(1)} %get-tuple-element.52), channel_id=1, source_target_pairs={{0,4},{4,8},{8,12},{12,16},{16,20},{20,24},{24,28},{28,32},{32,36}... | collective-permute-start | bytes 98312 | tf_op jit(solution)/shard_map/ppermute | solution.py:38
  2.1 8.0 %collective-permute-start.1 = (f32[2,8,4,128]{3,1,2,0:T(8,128)S(1)}, f32[2,8,4,128]{3,1,2,0:T(8,128)S(1)}, u32[]{:S(2)}, u32[]{:S(2)}) collective-permute-start(f32[2,8,4,128]{3,1,2,0:T(8,128)S(1)} %get-tuple-element.53), channel_id=1, source_target_pairs={{4,0},{8,4},{12,8},{16,12},{20,16},{24,20},{28,24},{32,28},{36,32}... | collective-permute-start | bytes 98312 | tf_op jit(solution)/shard_map/ppermute | solution.py:40
  10.3 2.6 %copy-start.1 = (bf16[1,2,32,1024]{3,2,1,0:T(8,128)(2,1)S(1)}, bf16[1,2,32,1024]{3,2,1,0:T(8,128)(2,1)}, u32[]{:S(2)}) copy-start(bf16[1,2,32,1024]{3,2,1,0:T(8,128)(2,1)} %param.7) | copy-start | bytes 393220
  10.3 2.6 %copy-start.3 = (bf16[1,32,1024]{2,1,0:T(8,128)(2,1)S(1)}, bf16[1,32,1024]{2,1,0:T(8,128)(2,1)}, u32[]{:S(2)}) copy-start(bf16[1,32,1024]{2,1,0:T(8,128)(2,1)} %param.6) | copy-start | bytes 196612
  10.3 2.7 %copy-start = (f32[1,2,8,64,128]{4,3,2,1,0:T(8,128)S(1)}, f32[1,2,8,64,128]{4,3,2,1,0:T(8,128)}, u32[]{:S(2)}) copy-start(f32[1,2,8,64,128]{4,3,2,1,0:T(8,128)} %param.5) | copy-start | bytes 1572868
  10.6 10.7 %collective-permute-start.2 = (f32[2,8,72,4]{2,1,3,0:T(8,128)S(1)}, f32[2,8,72,4]{2,1,3,0:T(8,128)S(1)}, u32[]{:S(2)}, u32[]{:S(2)}) collective-permute-start(f32[2,8,72,4]{2,1,3,0:T(8,128)S(1)} %copy.25), channel_id=1, source_target_pairs={{0,1},{1,2},{2,3},{3,0},{4,5},{5,6},{6,7},{7,4},{8,9},{9,10},{10,1... | collective-permute-start | bytes 55304 | tf_op jit(solution)/shard_map/ppermute | solution.py:38
  12.5 9.1 %collective-permute-start.3 = (f32[2,8,72,4]{2,1,3,0:T(8,128)S(1)}, f32[2,8,72,4]{2,1,3,0:T(8,128)S(1)}, u32[]{:S(2)}, u32[]{:S(2)}) collective-permute-start(f32[2,8,72,4]{2,1,3,0:T(8,128)S(1)} %copy.26), channel_id=1, source_target_pairs={{1,0},{2,1},{3,2},{0,3},{5,4},{6,5},{7,6},{4,7},{9,8},{10,9},{11,1... | collective-permute-start | bytes 55304 | tf_op jit(solution)/shard_map/ppermute | solution.py:40
  39.1 166.4 %copy-start.4 = (f32[1,32,1024]{2,1,0:T(8,128)S(1)}, f32[1,32,1024]{2,1,0:T(8,128)}, u32[]{:S(2)}) copy-start(f32[1,32,1024]{2,1,0:T(8,128)} %param.8) | copy-start | bytes 393220
  39.1 167.1 %copy-start.2 = (f32[1,2,32,1024]{3,2,1,0:T(8,128)S(1)}, f32[1,2,32,1024]{3,2,1,0:T(8,128)}, u32[]{:S(2)}) copy-start(f32[1,2,32,1024]{3,2,1,0:T(8,128)} %param.9) | copy-start | bytes 786436
  39.1 167.9 %collective-permute-start.4 = (f32[2,8,64,128]{3,2,1,0:T(8,128)S(1)}, f32[2,8,64,128]{3,2,1,0:T(8,128)S(1)}, u32[]{:S(2)}, u32[]{:S(2)}) collective-permute-start(f32[2,8,64,128]{3,2,1,0:T(8,128)S(1)} %copy.29), channel_id=1, source_target_pairs={{0,128},{1,129},{2,130},{3,131},{4,132},{5,133},{6,134},{7,135},{8... | collective-permute-start | bytes 1572872 | tf_op jit(solution)/shard_map/ppermute | solution.py:491

commit v2 on v1

--- a/solution.py
+++ b/solution.py
@@ -28,62 +28,11 @@
 E, U, W = 0, 1, 2
 
 
-def extended(cells, sides, width):
-    for axis, dim in sides:
-        count = lax.axis_size(axis)
-        head = lax.slice_in_dim(cells, 0, width, axis=dim)
-        tail = lax.slice_in_dim(cells, cells.shape[dim] - width, cells.shape[dim], axis=dim)
-        cells = jnp.concatenate(
-            [
-                lax.ppermute(tail, axis, [(i, (i + 1) % count) for i in range(count)]),
-                cells,
-                lax.ppermute(head, axis, [((i + 1) % count, i) for i in range(count)]),
-            ],
-            axis=dim,
-        )
-    return cells
-
-
-def react(padded):
-    center = padded[:, :, 1:-1, 1:-1]
-    below_plane = jnp.concatenate([center[:, :1], center[:, :-1]], axis=1)
-    above_plane = jnp.concatenate([center[:, 1:], center[:, -1:]], axis=1)
-    beside = below_plane + above_plane + padded[:, :, :-2, 1:-1] + padded[:, :, 2:, 1:-1]
-    beside = beside + padded[:, :, 1:-1, :-2] + padded[:, :, 1:-1, 2:]
-    laplace = beside - 6.0 * center
-    substrate = center[0]
-    catalyst = center[1]
-    growth = substrate * catalyst * catalyst
-    new_substrate = substrate + TIME_STEP * (
-        SUBSTRATE_DIFFUSION * laplace[0] - growth + FEED_RATE * (1.0 - substrate)
-    )
-    new_catalyst = catalyst + TIME_STEP * (
-        CATALYST_DIFFUSION * laplace[1] + growth - (FEED_RATE + KILL_RATE) * catalyst
-    )
-    return jnp.stack([new_substrate, new_catalyst])
-
-
-def to_blocks(brick):
-    extent = brick.shape
-    parts = brick.reshape(
-        extent[0], 2, extent[1] // 2, extent[2] // PATCH, PATCH, extent[3] // PATCH, PATCH
-    )
-    parts = parts.transpose(0, 1, 3, 5, 2, 4, 6)
-    return parts.reshape(4, OWN, COLS)
-
-
-def advance(cells):
-    padded = extended(cells, (("dp", 2), ("mp", 3)), STEPS)
-    for iteration in range(STEPS):
-        padded = react(padded)
-    return padded
-
-
 def kernel(
-    xs, ts, w, out,
-    wf, px, yd, tg, part, sbuf, rbuf, nf, dyf, act, slope, dhid, ered, dyred,
+    state, embed, mlp, out, state_out,
+    field, edge, edges, onehot, spread_in, xs, ts, wf, px, yd, tg, part, sbuf, rbuf, nf, dyf, act, slope, dhid, ered, dyred,
     acc, cs, cr, xs1, xr1, xs2, xr2, vsum, zs1, zr1, zs2, zr2,
-    role_s, role_r, x_s, x_r, ag_s, ag_r, rs_s, rs_r, mg_s, mg_r, gr_s, gr_r,
+    in_s, halo_s, halo_r, state_s, state_r, role_s, role_r, x_s, x_r, ag_s, ag_r, rs_s, rs_r, mg_s, mg_r, gr_s, gr_r,
 ):
     role = lax.axis_index("role")
     dp = lax.axis_index("dp")
@@ -97,17 +46,26 @@
     z1, z2 = z + 1 - 2 * (z % 2), (z + 2) % 4
     z3 = (z1 + 2) % 4
     c1 = 1 - c
+    zm = 3 - z
+    zl = jnp.where(role == 1, z, zm)
     to_c, to_x1, to_x3 = dev(x, z, c1), dev(x1, z, c), dev(x3, z, c)
     to_z1, to_z2 = dev(x, z1, c), dev(x, z2, c)
+    after, before = {"dp": (dp + 1) % 32}, {"dp": (dp + 31) % 32}
+    east, west = {"mp": (mp + 1) % 4}, {"mp": (mp + 3) % 4}
+    mirror = dev(x, zm, c)["dp"]
+    center = pltpu.make_async_copy(
+        state.at[0], field.at[0, :, :, pl.ds(8, 64), pl.ds(0, 128)], in_s.at[0]
+    )
+    center.start()
     other = [(mp + o) % 4 for o in range(4)]
 
     def at(start, size):
         return pl.ds(pl.multiple_of(start, 32), size)
 
     barrier = pltpu.get_barrier_semaphore()
-    friends = [to_c, to_x1, to_x3, to_z1, to_z2]
+    friends = [to_c, to_x1, to_x3, to_z1, to_z2, after, before, {"role": 1 - role}]
     friends += [{"mp": other[o]} for o in (1, 2, 3)]
-    friends += [{"role": 1 - role, "mp": other[o]} for o in range(4)]
+    friends += [{"role": 1 - role, "dp": mirror, "mp": other[o]} for o in range(4)]
     for friend in friends:
         pl.semaphore_signal(barrier, inc=1, device_id=friend, device_id_type=MESH)
     pl.semaphore_wait(barrier, len(friends))
@@ -127,29 +85,39 @@
     def arrive(dst, ssem, rsem, frm):
         copy(dst, dst, ssem, rsem, frm).wait_recv()
 
-    own_rows = at(c * 512 + x * 128 + z * 32, 32)
+    own_rows = at(c * 512 + x * 128 + zl * 32, 32)
+    far_rows = at(c * 512 + x * 128 + z * 32, 32)
+    w = (embed.at[0], mlp.at[0, 0], mlp.at[0, 1])
 
     def weights_across(k):
-        return copy(w.at[k], wf.at[k, own_rows], role_s.at[k], role_r.at[k], {"role": 0})
+        return copy(w[k], wf.at[k, far_rows], role_s.at[k], role_r.at[k], {"role": 0, "dp": mirror})
 
     def weights_here(k):
-        return pltpu.make_async_copy(w.at[k], wf.at[k, own_rows], role_r.at[k])
-
-    def patches(which, src, dst, base):
+        return pltpu.make_async_copy(w[k], wf.at[k, far_rows], role_r.at[k])
+
+    def patches(which, src, dst, base, o):
+        rows = at(base + 32 * mp, 32)
         made = []
-        for o in range(4):
-            rows = at(base + 32 * mp, 32)
-            for r in (1, 0):
-                if o == 0 and r == 0:
-                    continue
-                made.append(
-                    copy(src.at[other[o]], dst.at[rows], x_s.at[which, r, o], x_r.at[which, o],
-                         {"role": r, "mp": other[o]})
-                )
+        for r in (1, 0):
+            if o == 0 and r == 0:
+                continue
+            to = {"role": 1, "dp": mirror, "mp": other[o]} if r == 1 else {"role": 0, "mp": other[o]}
+            made.append(copy(src.at[other[o]], dst.at[rows], x_s.at[which, r, o], x_r.at[which, o], to))
         return made
 
     def patches_here(which, src, dst, base):
         return pltpu.make_async_copy(src.at[mp], dst.at[at(base + 32 * mp, 32)], x_r.at[which, 0])
+
+    def patches_go(which, src, dst, base):
+        @pl.when(role == 0)
+        def _():
+            for o in range(4):
+                for made in patches(which, src, dst, base, o):
+                    made.start()
+            patches_here(which, src, dst, base).start()
+
+    def final_state():
+        return copy(state_out, state_out, state_s.at[0], state_r.at[0], {"role": 1})
 
     @pl.when(role == 1)
     def _():
@@ -157,19 +125,93 @@
             weights_across(k).start()
             weights_here(k).start()
 
-    @pl.when(role == 0)
-    def _():
-        for made in patches(0, xs, px, 128):
-            made.start()
-        patches_here(0, xs, px, 128).start()
-        for made in patches(1, ts, tg, 0):
-            made.start()
-        patches_here(1, ts, tg, 0).start()
-
     def patches_arrive(which, dst, base):
         for o in range(4):
             frm = (mp + 4 - o) % 4
-            arrive(dst.at[at(base + 32 * frm, 32)], x_s.at[which, 1, o], x_r.at[which, o], {"mp": other[1]})
+            arrive(dst.at[at(base + 32 * frm, 32)], x_s.at[which, 1, o], x_r.at[which, o], east)
+
+    lane = lax.broadcasted_iota(jnp.int32, (80, 128), 1)
+
+    def halo_rows(i, src, dst, to):
+        ends = [field.at[0, :, :, pl.ds(start, 8), pl.ds(0, 128)] for start in (src, dst)]
+        return copy(ends[0], ends[1], halo_s.at[i], halo_r.at[i], to)
+
+    def rows_go():
+        for i, src, dst, to in ((0, 8, 72, before), (1, 64, 0, after)):
+            halo_rows(i, src, dst, to).start()
+
+    def columns_go():
+        halo_rows(0, 72, 72, after).wait_recv()
+        halo_rows(1, 0, 0, before).wait_recv()
+        halo_rows(0, 8, 72, before).wait_send()
+        halo_rows(1, 64, 0, after).wait_send()
+        edge[...] = jnp.zeros_like(edge)
+        for p in range(16):
+            cells = field[0, p // 8, p % 8, :, 0:128]
+            inside = (lane >= 4 * p) & (lane < 4 * p + 4)
+            edge[0] = jnp.where(inside, pltpu.roll(cells, 4 * p, 1) if p else cells, edge[0])
+            edge[1] = jnp.where(inside, pltpu.roll(cells, 4 * p + 4, 1), edge[1])
+        send(edge.at[0], edges.at[0], halo_s.at[2], halo_r.at[2], west)
+        send(edge.at[1], edges.at[1], halo_s.at[3], halo_r.at[3], east)
+
+    def columns_arrive():
+        arrive(edges.at[0], halo_s.at[2], halo_r.at[2], east)
+        arrive(edges.at[1], halo_s.at[3], halo_r.at[3], west)
+        for p in range(16):
+            behind = edges[0] if p == 0 else pltpu.roll(edges[0], 128 - 4 * p, 1)
+            ahead = pltpu.roll(edges[1], 124 - 4 * p, 1)
+            field[0, p // 8, p % 8, :, 128:256] = jnp.where(lane < 4, behind, jnp.where(lane >= 124, ahead, 0.0))
+
+    def advance(step):
+        now, later = step % 2, (step + 1) % 2
+
+        @pl.loop(0, 8)
+        def _(p):
+            low, high = jnp.maximum(p - 1, 0), jnp.minimum(p + 1, 7)
+
+            def laplace(s):
+                mid = field[now, s, p]
+                total = field[now, s, low] + field[now, s, high]
+                total = total + pltpu.roll(mid, 1, 0) + pltpu.roll(mid, 79, 0)
+                total = total + pltpu.roll(mid, 1, 1) + pltpu.roll(mid, 255, 1)
+                return mid, total - 6.0 * mid
+
+            substrate, first = laplace(0)
+            catalyst, second = laplace(1)
+            growth = substrate * catalyst * catalyst
+            field[later, 0, p] = substrate + TIME_STEP * (
+                SUBSTRATE_DIFFUSION * first - growth + FEED_RATE * (1.0 - substrate)
+            )
+            field[later, 1, p] = catalyst + TIME_STEP * (
+                CATALYST_DIFFUSION * second + growth - (FEED_RATE + KILL_RATE) * catalyst
+            )
+
+    def selection():
+        feature = lax.broadcasted_iota(jnp.int32, (128, 256), 1)
+        inner = lax.broadcasted_iota(jnp.int32, (128, 256), 0) % PATCH
+        for r in range(PATCH):
+            onehot[128 * r : 128 * r + 128, :] = jnp.where(feature == PATCH * r + inner, 1.0, 0.0).astype(BF16)
+
+    def to_patches(dst):
+        patch = lax.broadcasted_iota(jnp.int32, (8, 128), 0)
+        own = lax.broadcasted_iota(jnp.int32, (8, 128), 1) // PATCH == patch
+
+        @pl.loop(0, 4)
+        def _(j):
+            @pl.loop(0, 4)
+            def _(q):
+                species, plane = j // 2, 4 * (j % 2) + q
+                for r in range(PATCH):
+                    pieces = []
+                    for by in range(4):
+                        row = field[0, species, plane, pl.ds(8 + PATCH * by + r, 1), 0:128]
+                        pieces.append(jnp.where(own, jnp.broadcast_to(row, (8, 128)), 0.0))
+                    rows = pl.ds(pl.multiple_of(32 * q, 32), 32)
+                    spread_in[rows, 128 * r : 128 * r + 128] = jnp.concatenate(pieces, axis=0).astype(BF16)
+
+            moved = jnp.dot(spread_in[...], onehot[...], preferred_element_type=F32).astype(BF16)
+            for q in range(4):
+                dst[j, :, 256 * q : 256 * q + 256] = moved[32 * q : 32 * q + 32, :]
 
     def block(x_, z_=0, c_=c):
         return c_ * 512 + x_ * 128 + z_ * 32
@@ -181,18 +223,21 @@
     def g_arrive(k, i, start, size, frm):
         arrive(wf.at[k, at(start, size)], ag_s.at[k, i], ag_r.at[k, i], frm)
 
+    zl1, zl2 = zl + 1 - 2 * (zl % 2), (zl + 2) % 4
+    zl3 = (zl1 + 2) % 4
+
     def gather0(k):
         arrive(wf.at[k, own_rows], role_s.at[k], role_r.at[k], {"role": 1 - role})
-        g_send(k, 0, block(x, z), 32, to_z2)
-        g_send(k, 1, block(x, z), 32, to_z1)
+        g_send(k, 0, block(x, zl), 32, to_z2)
+        g_send(k, 1, block(x, zl), 32, to_z1)
 
     def gather1(k):
-        g_arrive(k, 0, block(x, z2), 32, to_z2)
-        g_send(k, 2, block(x, z2), 32, to_z1)
+        g_arrive(k, 0, block(x, zl2), 32, to_z2)
+        g_send(k, 2, block(x, zl2), 32, to_z1)
 
     def gather2(k):
-        g_arrive(k, 1, block(x, z1), 32, to_z1)
-        g_arrive(k, 2, block(x, z3), 32, to_z1)
+        g_arrive(k, 1, block(x, zl1), 32, to_z1)
+        g_arrive(k, 2, block(x, zl3), 32, to_z1)
         g_send(k, 3, block(x), 128, to_x1)
         g_send(k, 4, block(x), 128, to_x3)
         g_send(k, 7, block(x), 128, to_c)
@@ -337,15 +382,25 @@
         arrive(zr2.at[k], gr_s.at[k, 6], gr_r.at[k, 6], to_z2)
         out[k] = vsum[k, at(z * 32, 32), :] + zr1[k, 0].astype(F32) + zr2[k].astype(F32)
 
-    for k in (E, U, W):
-        gather0(k)
+    center.wait()
+    rows_go()
+    gather0(E)
+    selection()
+    to_patches(xs)
+    patches_go(0, xs, px, 128)
     gather1(E)
+    gather0(U)
+    columns_go()
     gather2(E)
     gather1(U)
+    gather0(W)
+    columns_arrive()
+    gather3(E)
+    advance(0)
+    gather4(E)
+    gather2(U)
     gather1(W)
-    gather3(E)
-    gather2(U)
-    gather4(E)
+    advance(1)
     gather5(E)
 
     patches_arrive(0, px, 128)
@@ -353,6 +408,7 @@
     partial_sums(0, xin, E)
     gather2(W)
     gather3(U)
+    advance(2)
     e = summed(0)
     recip = lax.rsqrt(jnp.mean(e * e, axis=1, keepdims=True) + 1e-06)
     ered[...] = e
@@ -360,6 +416,7 @@
     gather4(U)
     gather3(W)
     gather5(U)
+    advance(3)
     spread_arrive(0, nf, 0)
 
     def hidden(cols):
@@ -375,6 +432,14 @@
     gather4(W)
     gather5(W)
     partial_sums(1, act, W)
+    to_patches(ts)
+    patches_go(1, ts, tg, 0)
+
+    @pl.when(role == 0)
+    def _():
+        state_out[...] = field[0, :, :, 8:72, 0:128]
+        final_state().start()
+
     spread(1, yd, 0, (ered[...] + summed(1)).astype(BF16))
     patches_arrive(1, tg, 0)
     spread_arrive(1, yd, 0)
@@ -427,23 +492,33 @@
     def _():
         for k in (E, U, W):
             weights_across(k).wait_send()
+        final_state().wait_recv()
 
     @pl.when(role == 0)
     def _():
-        for made in patches(0, xs, px, 128) + patches(1, ts, tg, 0):
-            made.wait_send()
-
-
-def gradients(xs, ts, w):
+        for o in range(4):
+            for made in patches(0, xs, px, 128, o) + patches(1, ts, tg, 0, o):
+                made.wait_send()
+        final_state().wait_send()
+
+
+def train(state, embed, mlp):
     vmem = pl.BlockSpec(memory_space=pltpu.VMEM)
     dma = pltpu.SemaphoreType.DMA
     return pl.pallas_call(
         kernel,
         name="train",
-        out_shape=jax.ShapeDtypeStruct((3, OWN, COLS), F32),
-        in_specs=[vmem] * 3,
-        out_specs=vmem,
+        out_shape=(jax.ShapeDtypeStruct((3, OWN, COLS), F32), jax.ShapeDtypeStruct(state.shape[1:], F32)),
+        in_specs=[pl.BlockSpec(memory_space=pl.ANY), vmem, vmem],
+        out_specs=(vmem, vmem),
         scratch_shapes=[
+            pltpu.VMEM((2, 2, 8, 80, 256), F32),
+            pltpu.VMEM((2, 80, 128), F32),
+            pltpu.VMEM((2, 80, 128), F32),
+            pltpu.VMEM((2048, 256), BF16),
+            pltpu.VMEM((128, 2048), BF16),
+            pltpu.VMEM((4, OWN, COLS), BF16),
+            pltpu.VMEM((4, OWN, COLS), BF16),
             pltpu.VMEM((3, D, COLS), BF16),
             pltpu.VMEM((2 * ROWS, COLS), BF16),
             pltpu.VMEM((2 * ROWS, D), BF16),
@@ -470,6 +545,7 @@
             pltpu.VMEM((3, 2, OWN, COLS), BF16),
             pltpu.VMEM((3, OWN, COLS), BF16),
             pltpu.VMEM((3, OWN, COLS), BF16),
+            dma((1,)), dma((4,)), dma((4,)), dma((1,)), dma((1,)),
             dma((3,)), dma((3,)),
             dma((2, 2, 4)), dma((2, 4)),
             dma((3, 12)), dma((3, 12)),
@@ -481,20 +557,11 @@
             collective_id=0, has_side_effects=True, vmem_limit_bytes=52 * 1024 * 1024
         ),
         cost_estimate=pl.CostEstimate(flops=6 * 10**9, bytes_accessed=4 * 10**8, transcendentals=10**5),
-    )(xs, ts, w)
+    )(state, embed, mlp)
 
 
 def shards(state, embed, mlp, mom_embed, mom_mlp):
-    group_index = lax.axis_index("role")
-    start_cells = state[0]
-    cells = advance(start_cells)
-    arrived = lax.ppermute(cells, "role", [(0, 1)])
-    state_out = jnp.where(group_index == 0, cells, arrived)
-    grads = gradients(
-        to_blocks(start_cells.astype(BF16)),
-        to_blocks(cells.astype(BF16)),
-        jnp.concatenate([embed, mlp[0]], axis=0),
-    )
+    grads, state_out = train(state, embed, mlp)
     mom_embed_out = MOMENTUM_DECAY * mom_embed + grads[:1]
     mom_mlp_out = MOMENTUM_DECAY * mom_mlp + grads[None, 1:]
     embed_out = (embed.astype(F32) - LEARNING_RATE * mom_embed_out).astype(BF16)

time: 208 us -> 159 us (0.76)
  the two profiles are of different devices: /device:TPU:8 before, /device:TPU:136 now
where the time goes in v2:
time: 159 us
  Pallas kernels  153 us (96%)
  local copies, waits for them, and re-layouts  3.89 us (2%)
    pallas_call x1, Pallas kernels, train(): pl.pallas_call(kernel, name='train', out_shape=(jax.ShapeDtypeStruct((3,...  153 us
    unnamed x11, local copies, waits for them, and re-layouts  3.89 us

profile of v2, /device:TPU:136, one launch (start us, length us, event | category | flops | bytes accessed | tf_op | source)
XLA Modules:
  0.0 159.2 jit_solution(12243376567951548645)
XLA Ops:
  0.6 0.0 copy-start
  0.6 0.9 copy-done
  1.5 0.0 copy-start.1
  1.5 0.8 copy-done.1
  2.4 0.0 copy-start.2
  2.4 1.0 copy-done.2
  3.4 0.0 copy-start.4
  3.4 153.1 %train.1 = (f32[3,32,1024]{2,1,0:T(8,128)S(1)}, f32[2,8,64,128]{3,2,1,0:T(8,128)S(1)}) custom-call(f32[1,2,8,64,128]{4,3,2,1,0:T(8,128)S(1)} %copy-done.2, bf16[1,32,1024]{2,1,0:T(8,128)(2,1)S(1)} %copy-done.1, bf16[1,2,32,1024]{3,2,1,0:T(8,128)(2,1)S(1)} %copy-done), custom_call_target="tpu_custom_call" | custom-call | flops 6000000000 | bytes 400000000 | tf_op jit(solution)/shard_map/train/pallas_call | solution.py:508
  156.5 0.0 copy-done.4
  156.5 0.0 copy-start.3
  156.6 0.7 subtract_convert_fusion.1
  157.3 0.3 copy-done.3
  157.6 0.8 subtract_convert_fusion
  158.4 0.8 copy.11
Async XLA Ops:
  0.6 0.9 copy-start
  1.5 0.8 copy-start.1
  2.4 1.0 copy-start.2
  3.4 153.1 %copy-start.4 = (f32[1,32,1024]{2,1,0:T(8,128)S(1)}, f32[1,32,1024]{2,1,0:T(8,128)}, u32[]{:S(2)}) copy-start(f32[1,32,1024]{2,1,0:T(8,128)} %param.8) | copy-start | bytes 393220
  156.5 1.0 copy-start.3

commit v3 on v2

--- a/solution.py
+++ b/solution.py
@@ -30,7 +30,7 @@
 
 def kernel(
     state, embed, mlp, out, state_out,
-    field, edge, edges, onehot, spread_in, xs, ts, wf, px, yd, tg, part, sbuf, rbuf, nf, dyf, act, slope, dhid, ered, dyred,
+    field, passed, edge, edges, onehot, spread_in, xs, ts, wf, px, yd, tg, part, sbuf, rbuf, nf, dyf, act, slope, dhid, ered, dyred,
     acc, cs, cr, xs1, xr1, xs2, xr2, vsum, zs1, zr1, zs2, zr2,
     in_s, halo_s, halo_r, state_s, state_r, role_s, role_r, x_s, x_r, ag_s, ag_r, rs_s, rs_r, mg_s, mg_r, gr_s, gr_r,
 ):
@@ -63,7 +63,7 @@
         return pl.ds(pl.multiple_of(start, 32), size)
 
     barrier = pltpu.get_barrier_semaphore()
-    friends = [to_c, to_x1, to_x3, to_z1, to_z2, after, before, {"role": 1 - role}]
+    friends = [to_c, to_x1, to_x3, to_z1, to_z2, after, before, {"dp": mirror}]
     friends += [{"mp": other[o]} for o in (1, 2, 3)]
     friends += [{"role": 1 - role, "dp": mirror, "mp": other[o]} for o in range(4)]
     for friend in friends:
@@ -108,22 +108,49 @@
     def patches_here(which, src, dst, base):
         return pltpu.make_async_copy(src.at[mp], dst.at[at(base + 32 * mp, 32)], x_r.at[which, 0])
 
-    def patches_go(which, src, dst, base):
+    def patches_go(which, src, dst, base, some=(0, 1, 2, 3)):
         @pl.when(role == 0)
         def _():
-            for o in range(4):
+            for o in some:
                 for made in patches(which, src, dst, base, o):
                     made.start()
-            patches_here(which, src, dst, base).start()
-
-    def final_state():
-        return copy(state_out, state_out, state_s.at[0], state_r.at[0], {"role": 1})
+            if 0 in some:
+                patches_here(which, src, dst, base).start()
+
+    def state_part(whole, part):
+        return whole.at[part // 2, pl.ds(4 * (part % 2), 4)]
+
+    def state_across(part):
+        return copy(state_part(state_out, part), state_part(passed, part), state_s.at[part], state_r.at[part],
+                    {"role": 1, "dp": mirror})
+
+    def state_home(part):
+        return copy(state_part(passed, part), state_part(state_out, part), state_s.at[4 + part], state_r.at[4 + part],
+                    {"dp": mirror})
+
+    def state_go():
+        @pl.when(role == 0)
+        def _():
+            state_out[...] = field[0, :, :, 8:72, 0:128]
+            for part in range(4):
+                state_across(part).start()
+
+    def state_pass(part):
+        @pl.when(role == 1)
+        def _():
+            state_across(part).wait_recv()
+            state_home(part).start()
 
     @pl.when(role == 1)
     def _():
+        weights_across(E).start()
         for k in (E, U, W):
+            weights_here(k).start()
+
+    def weights_go(k):
+        @pl.when(role == 1)
+        def _():
             weights_across(k).start()
-            weights_here(k).start()
 
     def patches_arrive(which, dst, base):
         for o in range(4):
@@ -305,118 +332,157 @@
             rows = at(base + 32 * ((mp + 4 - o) % 4), 32)
             arrive(dst.at[rows], mg_s.at[i, o - 1], mg_r.at[i, o - 1], {"mp": other[o]})
 
-    def terms(k, lhs, rhs):
-        def product(rows, cols):
-            return lax.dot_general(lhs[:, rows], rhs[:, cols], (((0,), (0,)), ((), ())), preferred_element_type=F32)
+    pieces = {"W": (0, W, 0, COLS), "U": (1, U, 0, COLS), "E0": (2, E, 0, 512), "E1": (3, E, 512, 512)}
+
+    def product(piece, lhs, rhs, core, store):
+        _, _, first, width = pieces[piece]
 
         @pl.loop(0, 2)
         def _(t):
-            rows = pl.ds(pl.multiple_of(c1 * 512 + t * 256, 256), 256)
-            for s in (0, 1):
-                cols = pl.ds(512 * s, 512)
-                cs[k, pl.ds(pl.multiple_of(t * 256, 256), 256), cols] = product(rows, cols).astype(BF16)
-
-        send(cs.at[k], cr.at[k], gr_s.at[k, 0], gr_r.at[k, 0], to_c)
-
-        @pl.loop(0, 2)
-        def _(t):
-            rows = pl.ds(pl.multiple_of(c * 512 + t * 256, 256), 256)
-            for s in (0, 1):
-                cols = pl.ds(512 * s, 512)
-                acc[k, pl.ds(pl.multiple_of(t * 256, 256), 256), cols] = product(rows, cols)
+            rows = pl.ds(pl.multiple_of(core * 512 + t * 256, 256), 256)
+            local = pl.ds(pl.multiple_of(t * 256, 256), 256)
+            for start in range(first, first + width, 512):
+                cols = pl.ds(start, 512)
+                store(local, cols, lax.dot_general(
+                    lhs[:, rows], rhs[:, cols], (((0,), (0,)), ((), ())), preferred_element_type=F32
+                ))
+
+    def r_copy(piece, i, src, dst, to):
+        n = pieces[piece][0]
+        return copy(src, dst, gr_s.at[n, i], gr_r.at[n, i], to)
+
+    def r_send(piece, i, src, dst, to):
+        made = r_copy(piece, i, src, dst, to)
+        made.start()
+        started.append(made)
+
+    def terms_across(piece, lhs, rhs):
+        _, k, first, width = pieces[piece]
+
+        def store(local, cols, value):
+            cs[k, local, cols] = value.astype(BF16)
+
+        product(piece, lhs, rhs, c1, store)
+        whole = (k, slice(None), pl.ds(first, width))
+        r_send(piece, 0, cs.at[whole], cr.at[whole], to_c)
+
+    def terms_here(piece, lhs, rhs):
+        k = pieces[piece][1]
+
+        def store(local, cols, value):
+            acc[k, local, cols] = value
+
+        product(piece, lhs, rhs, c, store)
 
     def chunks(count, body):
         @pl.loop(0, count)
         def _(t):
             body(pl.multiple_of(t * 32, 32))
 
-    def pair(k, start):
-        return acc[k, pl.ds(start, 32), :] + cr[k, pl.ds(start, 32), :].astype(F32)
-
-    def reduce1(k):
-        arrive(cr.at[k], gr_s.at[k, 0], gr_r.at[k, 0], to_c)
+    def pair(k, start, cols):
+        return acc[k, pl.ds(start, 32), cols] + cr[k, pl.ds(start, 32), cols].astype(F32)
+
+    def reduce1(piece):
+        _, k, first, width = pieces[piece]
+        cols = pl.ds(first, width)
+        r_copy(piece, 0, cr.at[k, :, cols], cr.at[k, :, cols], to_c).wait_recv()
 
         def body(t):
             for h, far in ((0, x3), (1, x1)):
                 for i, xb in ((0, far), (1, x2)):
-                    xs1[k, h, i, pl.ds(t, 32), :] = pair(k, pl.multiple_of(xb * 128 + h * 64 + t, 32)).astype(BF16)
+                    value = pair(k, pl.multiple_of(xb * 128 + h * 64 + t, 32), cols)
+                    xs1[k, h, i, pl.ds(t, 32), cols] = value.astype(BF16)
 
         chunks(2, body)
-        send(xs1.at[k, 0], xr1.at[k, 0], gr_s.at[k, 1], gr_r.at[k, 1], to_x3)
-        send(xs1.at[k, 1], xr1.at[k, 1], gr_s.at[k, 2], gr_r.at[k, 2], to_x1)
-
-    def reduce2(k):
-        arrive(xr1.at[k, 0], gr_s.at[k, 1], gr_r.at[k, 1], to_x3)
-        arrive(xr1.at[k, 1], gr_s.at[k, 2], gr_r.at[k, 2], to_x1)
+        for h, to in ((0, to_x3), (1, to_x1)):
+            r_send(piece, 1 + h, xs1.at[k, h, :, :, cols], xr1.at[k, h, :, :, cols], to)
+
+    def reduce2(piece):
+        _, k, first, width = pieces[piece]
+        cols = pl.ds(first, width)
+        for h, frm in ((0, to_x3), (1, to_x1)):
+            r_copy(piece, 1 + h, xr1.at[k, h, :, :, cols], xr1.at[k, h, :, :, cols], frm).wait_recv()
 
         def body(t):
             for h, near in ((0, x1), (1, x3)):
-                value = pair(k, pl.multiple_of(near * 128 + h * 64 + t, 32)) + xr1[k, h, 1, pl.ds(t, 32), :].astype(F32)
-                xs2[k, h, pl.ds(t, 32), :] = value.astype(BF16)
+                value = pair(k, pl.multiple_of(near * 128 + h * 64 + t, 32), cols)
+                xs2[k, h, pl.ds(t, 32), cols] = (value + xr1[k, h, 1, pl.ds(t, 32), cols].astype(F32)).astype(BF16)
 
         chunks(2, body)
-        send(xs2.at[k, 0], xr2.at[k, 0], gr_s.at[k, 3], gr_r.at[k, 3], to_x1)
-        send(xs2.at[k, 1], xr2.at[k, 1], gr_s.at[k, 4], gr_r.at[k, 4], to_x3)
-
-    def reduce3(k):
-        arrive(xr2.at[k, 0], gr_s.at[k, 3], gr_r.at[k, 3], to_x1)
-        arrive(xr2.at[k, 1], gr_s.at[k, 4], gr_r.at[k, 4], to_x3)
+        for h, to in ((0, to_x1), (1, to_x3)):
+            r_send(piece, 3 + h, xs2.at[k, h, :, cols], xr2.at[k, h, :, cols], to)
+
+    def reduce3(piece):
+        _, k, first, width = pieces[piece]
+        cols = pl.ds(first, width)
+        for h, frm in ((0, to_x1), (1, to_x3)):
+            r_copy(piece, 3 + h, xr2.at[k, h, :, cols], xr2.at[k, h, :, cols], frm).wait_recv()
 
         def body(t):
             for h in (0, 1):
-                value = pair(k, pl.multiple_of(x * 128 + h * 64 + t, 32))
-                value = value + xr1[k, h, 0, pl.ds(t, 32), :].astype(F32) + xr2[k, h, pl.ds(t, 32), :].astype(F32)
-                vsum[k, pl.ds(pl.multiple_of(h * 64 + t, 32), 32), :] = value
+                value = pair(k, pl.multiple_of(x * 128 + h * 64 + t, 32), cols)
+                value = value + xr1[k, h, 0, pl.ds(t, 32), cols].astype(F32) + xr2[k, h, pl.ds(t, 32), cols].astype(F32)
+                vsum[k, pl.ds(pl.multiple_of(h * 64 + t, 32), 32), cols] = value
 
         chunks(2, body)
-        zs1[k, 0] = vsum[k, at(z1 * 32, 32), :].astype(BF16)
-        zs1[k, 1] = vsum[k, at(z3 * 32, 32), :].astype(BF16)
-        send(zs1.at[k], zr1.at[k], gr_s.at[k, 5], gr_r.at[k, 5], to_z1)
-
-    def reduce4(k):
-        arrive(zr1.at[k], gr_s.at[k, 5], gr_r.at[k, 5], to_z1)
-        zs2[k] = (vsum[k, at(z2 * 32, 32), :] + zr1[k, 1].astype(F32)).astype(BF16)
-        send(zs2.at[k], zr2.at[k], gr_s.at[k, 6], gr_r.at[k, 6], to_z2)
-
-    def reduce5(k):
-        arrive(zr2.at[k], gr_s.at[k, 6], gr_r.at[k, 6], to_z2)
-        out[k] = vsum[k, at(z * 32, 32), :] + zr1[k, 0].astype(F32) + zr2[k].astype(F32)
+        zs1[k, 0, :, cols] = vsum[k, at(z1 * 32, 32), cols].astype(BF16)
+        zs1[k, 1, :, cols] = vsum[k, at(z3 * 32, 32), cols].astype(BF16)
+        r_send(piece, 5, zs1.at[k, :, :, cols], zr1.at[k, :, :, cols], to_z1)
+
+    def reduce4(piece):
+        _, k, first, width = pieces[piece]
+        cols = pl.ds(first, width)
+        r_copy(piece, 5, zr1.at[k, :, :, cols], zr1.at[k, :, :, cols], to_z1).wait_recv()
+        zs2[k, :, cols] = (vsum[k, at(z2 * 32, 32), cols] + zr1[k, 1, :, cols].astype(F32)).astype(BF16)
+        r_send(piece, 6, zs2.at[k, :, cols], zr2.at[k, :, cols], to_z2)
+
+    def reduce5(piece):
+        _, k, first, width = pieces[piece]
+        cols = pl.ds(first, width)
+        r_copy(piece, 6, zr2.at[k, :, cols], zr2.at[k, :, cols], to_z2).wait_recv()
+        total = vsum[k, at(z * 32, 32), cols] + zr1[k, 0, :, cols].astype(F32)
+        out[k, :, cols] = total + zr2[k, :, cols].astype(F32)
 
     center.wait()
     rows_go()
-    gather0(E)
     selection()
     to_patches(xs)
-    patches_go(0, xs, px, 128)
+    gather0(E)
+    weights_go(U)
+    columns_go()
     gather1(E)
+    weights_go(W)
     gather0(U)
-    columns_go()
+    patches_go(0, xs, px, 128, (2, 0))
     gather2(E)
+    columns_arrive()
     gather1(U)
+    patches_go(0, xs, px, 128, (1, 3))
     gather0(W)
-    columns_arrive()
+    advance(0)
+    advance(1)
     gather3(E)
-    advance(0)
-    gather4(E)
     gather2(U)
     gather1(W)
-    advance(1)
+    advance(2)
+    advance(3)
+    gather4(E)
     gather5(E)
 
     patches_arrive(0, px, 128)
-    xin = px.at[128:256]
-    partial_sums(0, xin, E)
+    partial_sums(0, px.at[128:256], E)
+    gather3(U)
     gather2(W)
-    gather3(U)
-    advance(2)
+    to_patches(ts)
+    patches_go(1, ts, tg, 0)
+    state_go()
     e = summed(0)
     recip = lax.rsqrt(jnp.mean(e * e, axis=1, keepdims=True) + 1e-06)
     ered[...] = e
     spread(0, nf, 0, (e * recip).astype(BF16))
     gather4(U)
+    gather5(U)
     gather3(W)
-    gather5(U)
-    advance(3)
     spread_arrive(0, nf, 0)
 
     def hidden(cols):
@@ -432,14 +498,6 @@
     gather4(W)
     gather5(W)
     partial_sums(1, act, W)
-    to_patches(ts)
-    patches_go(1, ts, tg, 0)
-
-    @pl.when(role == 0)
-    def _():
-        state_out[...] = field[0, :, :, 8:72, 0:128]
-        final_state().start()
-
     spread(1, yd, 0, (ered[...] + summed(1)).astype(BF16))
     patches_arrive(1, tg, 0)
     spread_arrive(1, yd, 0)
@@ -450,40 +508,54 @@
 
     tiles(256, residual)
     partial_sums(2, px.at[0:128], E)
+    state_pass(0)
+    state_pass(1)
     dy = summed(2)
     dyred[...] = dy
     spread(2, dyf, 0, dy.astype(BF16))
+    state_pass(2)
+    state_pass(3)
     spread_arrive(2, dyf, 0)
+    terms_across("W", dyf, act)
+    terms_here("W", dyf, act)
 
     def hidden_back(cols):
         dhid[:, cols] = (with_cols(dyf[...], W, cols) * slope[:, cols]).astype(BF16)
 
+    reduce1("W")
     tiles(256, hidden_back)
     partial_sums(3, dhid, U)
-    terms(W, dyf, act)
+    terms_across("U", nf, dhid)
+    terms_here("U", nf, dhid)
     dn = summed(3)
     e = ered[...]
     recip = lax.rsqrt(jnp.mean(e * e, axis=1, keepdims=True) + 1e-06)
     de = dyred[...] + recip * dn - e * (recip * recip * recip) * jnp.mean(dn * e, axis=1, keepdims=True)
     spread(3, yd, 128, de.astype(BF16))
-    reduce1(W)
-    terms(U, nf, dhid)
+    reduce1("U")
+    reduce2("W")
     spread_arrive(3, yd, 128)
-    terms(E, yd, px)
-    reduce1(U)
-    reduce2(W)
-    reduce1(E)
-    reduce2(U)
-    reduce3(W)
-    reduce2(E)
-    reduce3(U)
-    reduce4(W)
-    reduce3(E)
-    reduce4(U)
-    reduce5(W)
-    reduce4(E)
-    reduce5(U)
-    reduce5(E)
+    terms_across("E0", yd, px)
+    terms_here("E0", yd, px)
+    terms_across("E1", yd, px)
+    reduce2("U")
+    reduce1("E0")
+    terms_here("E1", yd, px)
+    reduce1("E1")
+    reduce3("W")
+    reduce2("E0")
+    reduce2("E1")
+    reduce3("U")
+    reduce4("W")
+    reduce3("E0")
+    reduce4("U")
+    reduce3("E1")
+    reduce5("W")
+    reduce4("E0")
+    reduce4("E1")
+    reduce5("U")
+    reduce5("E0")
+    reduce5("E1")
 
     for made in started:
         made.wait_send()
@@ -492,14 +564,16 @@
     def _():
         for k in (E, U, W):
             weights_across(k).wait_send()
-        final_state().wait_recv()
+        for part in range(4):
+            state_home(part).wait()
 
     @pl.when(role == 0)
     def _():
         for o in range(4):
             for made in patches(0, xs, px, 128, o) + patches(1, ts, tg, 0, o):
                 made.wait_send()
-        final_state().wait_send()
+        for part in range(4):
+            state_across(part).wait_send()
 
 
 def train(state, embed, mlp):
@@ -509,10 +583,11 @@
         kernel,
         name="train",
         out_shape=(jax.ShapeDtypeStruct((3, OWN, COLS), F32), jax.ShapeDtypeStruct(state.shape[1:], F32)),
-        in_specs=[pl.BlockSpec(memory_space=pl.ANY), vmem, vmem],
+        in_specs=[pl.BlockSpec(memory_space=pltpu.HBM)] * 3,
         out_specs=(vmem, vmem),
         scratch_shapes=[
             pltpu.VMEM((2, 2, 8, 80, 256), F32),
+            pltpu.VMEM((2, 8, 64, 128), F32),
             pltpu.VMEM((2, 80, 128), F32),
             pltpu.VMEM((2, 80, 128), F32),
             pltpu.VMEM((2048, 256), BF16),
@@ -545,13 +620,13 @@
             pltpu.VMEM((3, 2, OWN, COLS), BF16),
             pltpu.VMEM((3, OWN, COLS), BF16),
             pltpu.VMEM((3, OWN, COLS), BF16),
-            dma((1,)), dma((4,)), dma((4,)), dma((1,)), dma((1,)),
+            dma((1,)), dma((4,)), dma((4,)), dma((8,)), dma((8,)),
             dma((3,)), dma((3,)),
             dma((2, 2, 4)), dma((2, 4)),
             dma((3, 12)), dma((3, 12)),
             dma((4, 3)), dma((4, 3)),
             dma((4, 3)), dma((4, 3)),
-            dma((3, 7)), dma((3, 7)),
+            dma((4, 7)), dma((4, 7)),
         ],
         compiler_params=pltpu.CompilerParams(
             collective_id=0, has_side_effects=True, vmem_limit_bytes=52 * 1024 * 1024

time: 159 us -> 130 us (0.82)
  the two profiles are of different devices: /device:TPU:136 before, /device:TPU:8 now
where the time goes in v3:
time: 130 us; the launch traced here: 129 us
  Pallas kernels  123 us (95%)
  local copies, waits for them, and re-layouts  3.89 us (3%)
  other arithmetic  1.5 us (1%)
    pallas_call x1, Pallas kernels, train(): pl.pallas_call(kernel, name='train', out_shape=(jax.ShapeDtypeStruct((3,...  123 us
    unnamed x11, local copies, waits for them, and re-layouts  3.89 us

profile of v3, /device:TPU:8, one launch (start us, length us, event | category | flops | bytes accessed | tf_op | source)
XLA Modules:
  0.0 129.3 jit_solution(16847909194350508047)
XLA Ops:
  0.6 0.0 copy-start
  0.6 0.9 copy-done
  1.5 0.0 copy-start.1
  1.5 0.8 copy-done.1
  2.4 0.0 copy-start.2
  2.4 1.0 copy-done.2
  3.4 0.0 copy-start.4
  3.4 123.2 %train.1 = (f32[3,32,1024]{2,1,0:T(8,128)S(1)}, f32[2,8,64,128]{3,2,1,0:T(8,128)S(1)}) custom-call(f32[1,2,8,64,128]{4,3,2,1,0:T(8,128)S(1)} %copy-done.2, bf16[1,32,1024]{2,1,0:T(8,128)(2,1)S(1)} %copy-done.1, bf16[1,2,32,1024]{3,2,1,0:T(8,128)(2,1)S(1)} %copy-done), custom_call_target="tpu_custom_call" | custom-call | flops 6000000000 | bytes 400000000 | tf_op jit(solution)/shard_map/train/pallas_call | solution.py:582
  126.7 0.0 copy-done.4
  126.7 0.0 copy-start.3
  126.7 0.7 subtract_convert_fusion.1
  127.4 0.3 copy-done.3
  127.7 0.8 subtract_convert_fusion
  128.5 0.8 copy.11
Async XLA Ops:
  0.6 0.9 copy-start
  1.5 0.8 copy-start.1
  2.4 1.0 copy-start.2
  3.4 123.3 %copy-start.4 = (f32[1,32,1024]{2,1,0:T(8,128)S(1)}, f32[1,32,1024]{2,1,0:T(8,128)}, u32[]{:S(2)}) copy-start(f32[1,32,1024]{2,1,0:T(8,128)} %param.8) | copy-start | bytes 393220
  126.7 1.0 copy-start.3

commit v4 on v3

--- a/solution.py
+++ b/solution.py
@@ -30,7 +30,7 @@
 
 def kernel(
     state, embed, mlp, out, state_out,
-    field, passed, edge, edges, onehot, spread_in, xs, ts, wf, px, yd, tg, part, sbuf, rbuf, nf, dyf, act, slope, dhid, ered, dyred,
+    total_rows, field, passed, edge, edges, onehot, spread_in, xs, ts, wf, px, yd, tg, part, sbuf, rbuf, nf, dyf, act, slope, dhid, ered, dyred,
     acc, cs, cr, xs1, xr1, xs2, xr2, vsum, zs1, zr1, zs2, zr2,
     in_s, halo_s, halo_r, state_s, state_r, role_s, role_r, x_s, x_r, ag_s, ag_r, rs_s, rs_r, mg_s, mg_r, gr_s, gr_r,
 ):
@@ -60,10 +60,10 @@
     other = [(mp + o) % 4 for o in range(4)]
 
     def at(start, size):
-        return pl.ds(pl.multiple_of(start, 32), size)
+        return pl.ds(pl.multiple_of(start, 16), size)
 
     barrier = pltpu.get_barrier_semaphore()
-    friends = [to_c, to_x1, to_x3, to_z1, to_z2, after, before, {"dp": mirror}]
+    friends = [to_c, to_x1, to_x3, to_z1, to_z2, after, before, {"dp": mirror}, {"role": 1 - role}]
     friends += [{"mp": other[o]} for o in (1, 2, 3)]
     friends += [{"role": 1 - role, "dp": mirror, "mp": other[o]} for o in range(4)]
     for friend in friends:
@@ -84,6 +84,12 @@
 
     def arrive(dst, ssem, rsem, frm):
         copy(dst, dst, ssem, rsem, frm).wait_recv()
+
+    def post(src, dst, ssem, rsem, to):
+        copy(src, dst, ssem, rsem, to).start()
+
+    def all_posted(whole, ssem):
+        pltpu.make_async_copy(whole, whole, ssem).wait()
 
     own_rows = at(c * 512 + x * 128 + zl * 32, 32)
     far_rows = at(c * 512 + x * 128 + z * 32, 32)
@@ -102,11 +108,11 @@
             if o == 0 and r == 0:
                 continue
             to = {"role": 1, "dp": mirror, "mp": other[o]} if r == 1 else {"role": 0, "mp": other[o]}
-            made.append(copy(src.at[other[o]], dst.at[rows], x_s.at[which, r, o], x_r.at[which, o], to))
+            made.append(copy(src.at[other[o]], dst.at[rows], x_s.at[which], x_r.at[which], to))
         return made
 
     def patches_here(which, src, dst, base):
-        return pltpu.make_async_copy(src.at[mp], dst.at[at(base + 32 * mp, 32)], x_r.at[which, 0])
+        return pltpu.make_async_copy(src.at[mp], dst.at[at(base + 32 * mp, 32)], x_r.at[which])
 
     def patches_go(which, src, dst, base, some=(0, 1, 2, 3)):
         @pl.when(role == 0)
@@ -120,20 +126,26 @@
     def state_part(whole, part):
         return whole.at[part // 2, pl.ds(4 * (part % 2), 4)]
 
+    def final_part(part):
+        return field.at[0, part // 2, pl.ds(4 * (part % 2), 4), pl.ds(8, 64), pl.ds(0, 128)]
+
     def state_across(part):
-        return copy(state_part(state_out, part), state_part(passed, part), state_s.at[part], state_r.at[part],
+        return copy(final_part(part), state_part(passed, part), state_s.at[part], state_r.at[part],
                     {"role": 1, "dp": mirror})
+
+    def state_here(part):
+        return pltpu.make_async_copy(final_part(part), state_part(state_out, part), in_s.at[1 + part])
 
     def state_home(part):
         return copy(state_part(passed, part), state_part(state_out, part), state_s.at[4 + part], state_r.at[4 + part],
                     {"dp": mirror})
 
-    def state_go():
+    def state_go(first):
         @pl.when(role == 0)
         def _():
-            state_out[...] = field[0, :, :, 8:72, 0:128]
-            for part in range(4):
+            for part in (first, first + 1):
                 state_across(part).start()
+                state_here(part).start()
 
     def state_pass(part):
         @pl.when(role == 1)
@@ -153,9 +165,7 @@
             weights_across(k).start()
 
     def patches_arrive(which, dst, base):
-        for o in range(4):
-            frm = (mp + 4 - o) % 4
-            arrive(dst.at[at(base + 32 * frm, 32)], x_s.at[which, 1, o], x_r.at[which, o], east)
+        arrive(dst.at[base : base + 128], x_s.at[which], x_r.at[which], east)
 
     lane = lax.broadcasted_iota(jnp.int32, (80, 128), 1)
 
@@ -240,55 +250,56 @@
             for q in range(4):
                 dst[j, :, 256 * q : 256 * q + 256] = moved[32 * q : 32 * q + 32, :]
 
-    def block(x_, z_=0, c_=c):
-        return c_ * 512 + x_ * 128 + z_ * 32
+    zl1, zl2 = zl + 1 - 2 * (zl % 2), (zl + 2) % 4
+    label = (zl, zl2, zl1, (zl1 + 2) % 4)
+
+    def block(x_, b, c_=c):
+        return c_ * 512 + x_ * 128 + label[b] * 32
 
     def g_send(k, i, start, size, to):
         rows = at(start, size)
-        send(wf.at[k, rows], wf.at[k, rows], ag_s.at[k, i], ag_r.at[k, i], to)
+        post(wf.at[k, rows], wf.at[k, rows], ag_s.at[k], ag_r.at[k, i], to)
 
     def g_arrive(k, i, start, size, frm):
-        arrive(wf.at[k, at(start, size)], ag_s.at[k, i], ag_r.at[k, i], frm)
-
-    zl1, zl2 = zl + 1 - 2 * (zl % 2), (zl + 2) % 4
-    zl3 = (zl1 + 2) % 4
+        arrive(wf.at[k, at(start, size)], ag_s.at[k], ag_r.at[k, i], frm)
+
+    def along_x(k, b):
+        g_send(k, 3 + b, block(x, b), 32, to_x1)
+        g_send(k, 7 + b, block(x, b), 32, to_x3)
+        g_send(k, 12, block(x, b), 32, to_c)
 
     def gather0(k):
         arrive(wf.at[k, own_rows], role_s.at[k], role_r.at[k], {"role": 1 - role})
-        g_send(k, 0, block(x, zl), 32, to_z2)
-        g_send(k, 1, block(x, zl), 32, to_z1)
+        g_send(k, 0, block(x, 0), 32, to_z2)
+        g_send(k, 1, block(x, 0), 32, to_z1)
+        along_x(k, 0)
 
     def gather1(k):
-        g_arrive(k, 0, block(x, zl2), 32, to_z2)
-        g_send(k, 2, block(x, zl2), 32, to_z1)
+        g_arrive(k, 0, block(x, 1), 32, to_z2)
+        g_send(k, 2, block(x, 1), 32, to_z1)
+        along_x(k, 1)
 
     def gather2(k):
-        g_arrive(k, 1, block(x, zl1), 32, to_z1)
-        g_arrive(k, 2, block(x, zl3), 32, to_z1)
-        g_send(k, 3, block(x), 128, to_x1)
-        g_send(k, 4, block(x), 128, to_x3)
-        g_send(k, 7, block(x), 128, to_c)
-
-    def gather3(k):
-        g_arrive(k, 3, block(x1), 128, to_x1)
-        g_send(k, 5, block(x1), 64, to_x3)
-        g_send(k, 8, block(x1), 128, to_c)
-        g_arrive(k, 4, block(x3), 128, to_x3)
-        g_send(k, 6, block(x3) + 64, 64, to_x1)
-        g_send(k, 9, block(x3), 128, to_c)
+        g_arrive(k, 1, block(x, 2), 32, to_z1)
+        along_x(k, 2)
+        g_arrive(k, 2, block(x, 3), 32, to_z1)
+        along_x(k, 3)
+
+    def gather3(k, some):
+        for b in some:
+            g_arrive(k, 3 + b, block(x1, b), 32, to_x1)
+            g_send(k, 11, block(x1, b), 16, to_x3)
+            g_send(k, 12, block(x1, b), 32, to_c)
+            g_arrive(k, 7 + b, block(x3, b), 32, to_x3)
+            g_send(k, 11, block(x3, b) + 16, 16, to_x1)
+            g_send(k, 12, block(x3, b), 32, to_c)
 
     def gather4(k):
-        g_arrive(k, 5, block(x2), 64, to_x3)
-        g_send(k, 10, block(x2), 64, to_c)
-        g_arrive(k, 6, block(x2) + 64, 64, to_x1)
-        g_send(k, 11, block(x2) + 64, 64, to_c)
+        g_arrive(k, 11, c * 512 + x2 * 128, 128, to_x1)
+        g_send(k, 12, c * 512 + x2 * 128, 128, to_c)
 
     def gather5(k):
-        g_arrive(k, 7, block(x, 0, c1), 128, to_c)
-        g_arrive(k, 8, block(x1, 0, c1), 128, to_c)
-        g_arrive(k, 9, block(x3, 0, c1), 128, to_c)
-        g_arrive(k, 10, block(x2, 0, c1), 64, to_c)
-        g_arrive(k, 11, block(x2, 0, c1) + 64, 64, to_c)
+        g_arrive(k, 12, c1 * 512, 512, to_c)
 
     def tiles(width, body):
         @pl.loop(0, COLS // width)
@@ -303,49 +314,62 @@
 
     mine = at(32 * mp, 32)
 
+    def half(s):
+        return pl.ds(512 * s, 512)
+
     def partial_sums(i, lhs, k):
-        def body(cols):
-            value = with_rows(lhs[...], k, cols)
-            part[:, cols] = value
-            sbuf[i, :, cols] = value.astype(BF16)
-
-        tiles(256, body)
+        for s in (0, 1):
+
+            @pl.loop(0, 2)
+            def _(t):
+                cols = pl.ds(pl.multiple_of(512 * s + 256 * t, 256), 256)
+                value = with_rows(lhs[...], k, cols)
+                part[:, cols] = value
+                sbuf[i, :, cols] = value.astype(BF16)
+
+            for o in (2, 1, 3):
+                post(sbuf.at[i, at(32 * other[o], 32), half(s)], rbuf.at[i, o - 1, :, half(s)],
+                     rs_s.at[0], rs_r.at[i, s], {"mp": other[o]})
+
+    def summed(i, s):
+        total = part[mine, half(s)]
+        arrive(rbuf.at[i, :, :, half(s)], rs_s.at[0], rs_r.at[i, s], east)
+        for o in (1, 2, 3):
+            total = total + rbuf[i, o - 1, :, half(s)].astype(F32)
+        return total
+
+    def all_summed(i):
+        return jnp.concatenate([summed(i, 0), summed(i, 1)], axis=1)
+
+    def spread(i, s, dst, base, value):
+        rows = at(base + 32 * mp, 32)
+        dst[rows, half(s)] = value
         for o in (2, 1, 3):
-            send(sbuf.at[i, at(32 * other[o], 32)], rbuf.at[i, o - 1], rs_s.at[i, o - 1], rs_r.at[i, o - 1],
-                 {"mp": other[o]})
-
-    def summed(i):
-        total = part[mine, :]
-        for o in (1, 3, 2):
-            arrive(rbuf.at[i, o - 1], rs_s.at[i, o - 1], rs_r.at[i, o - 1], {"mp": other[o]})
-            total = total + rbuf[i, o - 1].astype(F32)
-        return total
-
-    def spread(i, dst, base, value):
-        rows = at(base + 32 * mp, 32)
-        dst[rows, :] = value
-        for o in (2, 1, 3):
-            send(dst.at[rows], dst.at[rows], mg_s.at[i, o - 1], mg_r.at[i, o - 1], {"mp": other[o]})
+            post(dst.at[rows, half(s)], dst.at[rows, half(s)], mg_s.at[0], mg_r.at[i], {"mp": other[o]})
+
+    def spread_all(i, dst, base, value):
+        for s in (0, 1):
+            spread(i, s, dst, base, value[:, 512 * s : 512 * s + 512])
 
     def spread_arrive(i, dst, base):
-        for o in (1, 3, 2):
-            rows = at(base + 32 * ((mp + 4 - o) % 4), 32)
-            arrive(dst.at[rows], mg_s.at[i, o - 1], mg_r.at[i, o - 1], {"mp": other[o]})
-
-    pieces = {"W": (0, W, 0, COLS), "U": (1, U, 0, COLS), "E0": (2, E, 0, 512), "E1": (3, E, 512, 512)}
+        arrive(dst.at[base : base + 96], mg_s.at[0], mg_r.at[i], east)
+
+    pieces = {"W": (0, W, 0, 512), "U": (1, U, 0, 512), "E0": (2, E, 0, 512), "E1": (3, E, 512, 512)}
+
+    def in_matrix(group, k, first, width):
+        return pl.ds(first, width) if k == E else pl.ds(pl.multiple_of(512 * group + first, 512), width)
 
     def product(piece, lhs, rhs, core, store):
-        _, _, first, width = pieces[piece]
+        _, k, first, width = pieces[piece]
 
         @pl.loop(0, 2)
         def _(t):
             rows = pl.ds(pl.multiple_of(core * 512 + t * 256, 256), 256)
             local = pl.ds(pl.multiple_of(t * 256, 256), 256)
-            for start in range(first, first + width, 512):
-                cols = pl.ds(start, 512)
-                store(local, cols, lax.dot_general(
-                    lhs[:, rows], rhs[:, cols], (((0,), (0,)), ((), ())), preferred_element_type=F32
-                ))
+            store(local, pl.ds(first, width), lax.dot_general(
+                lhs[:, rows], rhs[:, in_matrix(role, k, first, width)], (((0,), (0,)), ((), ())),
+                preferred_element_type=F32,
+            ))
 
     def r_copy(piece, i, src, dst, to):
         n = pieces[piece][0]
@@ -436,12 +460,28 @@
         zs2[k, :, cols] = (vsum[k, at(z2 * 32, 32), cols] + zr1[k, 1, :, cols].astype(F32)).astype(BF16)
         r_send(piece, 6, zs2.at[k, :, cols], zr2.at[k, :, cols], to_z2)
 
+    def result(piece):
+        n, k, first, width = pieces[piece]
+        part = (k, slice(None), pl.ds(first, width) if k == E else slice(None))
+        return pltpu.make_async_copy(total_rows.at[part], out.at[part], in_s.at[5 + n])
+
     def reduce5(piece):
         _, k, first, width = pieces[piece]
         cols = pl.ds(first, width)
         r_copy(piece, 6, zr2.at[k, :, cols], zr2.at[k, :, cols], to_z2).wait_recv()
         total = vsum[k, at(z * 32, 32), cols] + zr1[k, 0, :, cols].astype(F32)
-        out[k, :, cols] = total + zr2[k, :, cols].astype(F32)
+        here = total_rows.at[k, :, in_matrix(role, k, first, width)]
+        here[...] = total + zr2[k, :, cols].astype(F32)
+        if k != E:
+            r_send(piece, 7, here, here, {"role": 1 - role})
+        else:
+            result(piece).start()
+
+    def reduced(piece):
+        _, k, first, width = pieces[piece]
+        there = total_rows.at[k, :, in_matrix(1 - role, k, first, width)]
+        r_copy(piece, 7, there, there, {"role": 1 - role}).wait_recv()
+        result(piece).start()
 
     center.wait()
     rows_go()
@@ -449,40 +489,43 @@
     to_patches(xs)
     gather0(E)
     weights_go(U)
+    patches_go(0, xs, px, 128, (2, 0))
     columns_go()
     gather1(E)
     weights_go(W)
+    patches_go(0, xs, px, 128, (1, 3))
     gather0(U)
-    patches_go(0, xs, px, 128, (2, 0))
+    gather3(E, (0,))
     gather2(E)
     columns_arrive()
+    gather3(E, (1,))
+    advance(0)
     gather1(U)
-    patches_go(0, xs, px, 128, (1, 3))
     gather0(W)
-    advance(0)
     advance(1)
-    gather3(E)
+    gather3(E, (2, 3))
     gather2(U)
+    advance(2)
     gather1(W)
-    advance(2)
     advance(3)
+    gather3(U, (0, 1))
     gather4(E)
+    to_patches(ts)
+    patches_go(1, ts, tg, 0)
     gather5(E)
 
     patches_arrive(0, px, 128)
     partial_sums(0, px.at[128:256], E)
-    gather3(U)
+    gather3(U, (2, 3))
     gather2(W)
-    to_patches(ts)
-    patches_go(1, ts, tg, 0)
-    state_go()
-    e = summed(0)
+    gather3(W, (0, 1))
+    e = all_summed(0)
     recip = lax.rsqrt(jnp.mean(e * e, axis=1, keepdims=True) + 1e-06)
     ered[...] = e
-    spread(0, nf, 0, (e * recip).astype(BF16))
+    spread_all(0, nf, 0, (e * recip).astype(BF16))
     gather4(U)
+    gather3(W, (2, 3))
     gather5(U)
-    gather3(W)
     spread_arrive(0, nf, 0)
 
     def hidden(cols):
@@ -498,7 +541,9 @@
     gather4(W)
     gather5(W)
     partial_sums(1, act, W)
-    spread(1, yd, 0, (ered[...] + summed(1)).astype(BF16))
+    state_go(0)
+    for s in (0, 1):
+        spread(1, s, yd, 0, (ered[:, half(s)] + summed(1, s)).astype(BF16))
     patches_arrive(1, tg, 0)
     spread_arrive(1, yd, 0)
 
@@ -508,13 +553,13 @@
 
     tiles(256, residual)
     partial_sums(2, px.at[0:128], E)
+    state_go(2)
+    for s in (0, 1):
+        dy = summed(2, s)
+        dyred[:, half(s)] = dy
+        spread(2, s, dyf, 0, dy.astype(BF16))
     state_pass(0)
     state_pass(1)
-    dy = summed(2)
-    dyred[...] = dy
-    spread(2, dyf, 0, dy.astype(BF16))
-    state_pass(2)
-    state_pass(3)
     spread_arrive(2, dyf, 0)
     terms_across("W", dyf, act)
     terms_here("W", dyf, act)
@@ -525,40 +570,50 @@
     reduce1("W")
     tiles(256, hidden_back)
     partial_sums(3, dhid, U)
+    state_pass(2)
+    state_pass(3)
     terms_across("U", nf, dhid)
     terms_here("U", nf, dhid)
-    dn = summed(3)
+    reduce1("U")
+    reduce2("W")
+    dn = all_summed(3)
     e = ered[...]
     recip = lax.rsqrt(jnp.mean(e * e, axis=1, keepdims=True) + 1e-06)
     de = dyred[...] + recip * dn - e * (recip * recip * recip) * jnp.mean(dn * e, axis=1, keepdims=True)
-    spread(3, yd, 128, de.astype(BF16))
-    reduce1("U")
-    reduce2("W")
+    spread_all(3, yd, 128, de.astype(BF16))
+    reduce3("W")
+    reduce2("U")
     spread_arrive(3, yd, 128)
     terms_across("E0", yd, px)
+    terms_across("E1", yd, px)
+    reduce4("W")
+    reduce3("U")
     terms_here("E0", yd, px)
-    terms_across("E1", yd, px)
-    reduce2("U")
+    terms_here("E1", yd, px)
     reduce1("E0")
-    terms_here("E1", yd, px)
     reduce1("E1")
-    reduce3("W")
+    reduce5("W")
+    reduce4("U")
     reduce2("E0")
     reduce2("E1")
-    reduce3("U")
-    reduce4("W")
+    reduce5("U")
     reduce3("E0")
-    reduce4("U")
     reduce3("E1")
-    reduce5("W")
     reduce4("E0")
     reduce4("E1")
-    reduce5("U")
+    reduced("W")
+    reduced("U")
     reduce5("E0")
     reduce5("E1")
 
     for made in started:
         made.wait_send()
+    for k in (E, U, W):
+        all_posted(wf.at[k, 0:992], ag_s.at[k])
+    all_posted(sbuf.at[0:3], rs_s.at[0])
+    all_posted(sbuf.at[0:3], mg_s.at[0])
+    for piece in pieces:
+        result(piece).wait()
 
     @pl.when(role == 1)
     def _():
@@ -569,23 +624,23 @@
 
     @pl.when(role == 0)
     def _():
-        for o in range(4):
-            for made in patches(0, xs, px, 128, o) + patches(1, ts, tg, 0, o):
-                made.wait_send()
+        for which in (0, 1):
+            all_posted(px.at[0:224], x_s.at[which])
         for part in range(4):
             state_across(part).wait_send()
+            state_here(part).wait()
 
 
 def train(state, embed, mlp):
-    vmem = pl.BlockSpec(memory_space=pltpu.VMEM)
     dma = pltpu.SemaphoreType.DMA
     return pl.pallas_call(
         kernel,
         name="train",
         out_shape=(jax.ShapeDtypeStruct((3, OWN, COLS), F32), jax.ShapeDtypeStruct(state.shape[1:], F32)),
         in_specs=[pl.BlockSpec(memory_space=pltpu.HBM)] * 3,
-        out_specs=(vmem, vmem),
+        out_specs=(pl.BlockSpec(memory_space=pl.ANY), pl.BlockSpec(memory_space=pl.ANY)),
         scratch_shapes=[
+            pltpu.VMEM((3, OWN, COLS), F32),
             pltpu.VMEM((2, 2, 8, 80, 256), F32),
             pltpu.VMEM((2, 8, 64, 128), F32),
             pltpu.VMEM((2, 80, 128), F32),
@@ -620,13 +675,13 @@
             pltpu.VMEM((3, 2, OWN, COLS), BF16),
             pltpu.VMEM((3, OWN, COLS), BF16),
             pltpu.VMEM((3, OWN, COLS), BF16),
-            dma((1,)), dma((4,)), dma((4,)), dma((8,)), dma((8,)),
+            dma((9,)), dma((4,)), dma((4,)), dma((8,)), dma((8,)),
             dma((3,)), dma((3,)),
-            dma((2, 2, 4)), dma((2, 4)),
-            dma((3, 12)), dma((3, 12)),
-            dma((4, 3)), dma((4, 3)),
-            dma((4, 3)), dma((4, 3)),
-            dma((4, 7)), dma((4, 7)),
+            dma((2,)), dma((2,)),
+            dma((3,)), dma((3, 13)),
+            dma((1,)), dma((4, 2)),
+            dma((1,)), dma((4,)),
+            dma((4, 8)), dma((4, 8)),
         ],
         compiler_params=pltpu.CompilerParams(
             collective_id=0, has_side_effects=True, vmem_limit_bytes=52 * 1024 * 1024

time: 130 us -> 114 us (0.88)
  Pallas kernels: 123 us -> 108 us
    pallas_call x1, Pallas kernels: 123 us -> 108 us  [train(): pl.pallas_call(kernel, name='train', out_shape=(jax.ShapeDtypeStruct((3,...]
where the time goes in v4:
time: 114 us
  Pallas kernels  108 us (95%)
  local copies, waits for them, and re-layouts  3.89 us (3%)
  other arithmetic  1.5 us (1%)
    pallas_call x1, Pallas kernels, train(): pl.pallas_call(kernel, name='train', out_shape=(jax.ShapeDtypeStruct((3,...  108 us
    unnamed x11, local copies, waits for them, and re-layouts  3.89 us

profile of v4, /device:TPU:8, one launch (start us, length us, event | category | flops | bytes accessed | tf_op | source)
XLA Modules:
  0.0 113.6 jit_solution(5338261788929325145)
XLA Ops:
  0.6 0.0 copy-start
  0.6 0.9 copy-done
  1.5 0.0 copy-start.1
  1.5 0.8 copy-done.1
  2.4 0.0 copy-start.2
  2.4 1.0 copy-done.2
  3.4 0.0 copy-start.4
  3.4 107.5 %train.1 = (f32[3,32,1024]{2,1,0:T(8,128)S(1)}, f32[2,8,64,128]{3,2,1,0:T(8,128)S(1)}) custom-call(f32[1,2,8,64,128]{4,3,2,1,0:T(8,128)S(1)} %copy-done.2, bf16[1,32,1024]{2,1,0:T(8,128)(2,1)S(1)} %copy-done.1, bf16[1,2,32,1024]{3,2,1,0:T(8,128)(2,1)S(1)} %copy-done), custom_call_target="tpu_custom_call" | custom-call | flops 6000000000 | bytes 400000000 | tf_op jit(solution)/shard_map/train/pallas_call | solution.py:636
  111.0 0.0 copy-done.4
  111.0 0.0 copy-start.3
  111.0 0.7 subtract_convert_fusion.1
  111.7 0.3 copy-done.3
  112.0 0.8 subtract_convert_fusion
  112.8 0.8 copy.11
Async XLA Ops:
  0.6 0.9 copy-start
  1.5 0.8 copy-start.1
  2.4 1.0 copy-start.2
  3.4 107.6 %copy-start.4 = (f32[1,32,1024]{2,1,0:T(8,128)S(1)}, f32[1,32,1024]{2,1,0:T(8,128)}, u32[]{:S(2)}) copy-start(f32[1,32,1024]{2,1,0:T(8,128)} %param.8) | copy-start | bytes 393220
  111.0 1.0 copy-start.3

commit v5 on v4

--- a/solution.py
+++ b/solution.py
@@ -354,7 +354,9 @@
     def spread_arrive(i, dst, base):
         arrive(dst.at[base : base + 96], mg_s.at[0], mg_r.at[i], east)
 
-    pieces = {"W": (0, W, 0, 512), "U": (1, U, 0, 512), "E0": (2, E, 0, 512), "E1": (3, E, 512, 512)}
+    pieces = {"W": (0, W, 0, 512), "U": (1, U, 0, 512)}
+    parts = ("E0", "E1", "E2", "E3")
+    pieces.update({name: (2 + i, E, 256 * i, 256) for i, name in enumerate(parts)})
 
     def in_matrix(group, k, first, width):
         return pl.ds(first, width) if k == E else pl.ds(pl.multiple_of(512 * group + first, 512), width)
@@ -373,12 +375,16 @@
 
     def r_copy(piece, i, src, dst, to):
         n = pieces[piece][0]
-        return copy(src, dst, gr_s.at[n, i], gr_r.at[n, i], to)
+        return copy(src, dst, gr_s.at[n if i < 7 else 6 + n], gr_r.at[n, i], to)
 
     def r_send(piece, i, src, dst, to):
-        made = r_copy(piece, i, src, dst, to)
-        made.start()
-        started.append(made)
+        r_copy(piece, i, src, dst, to).start()
+
+    def r_posted(piece):
+        n, k, first, width = pieces[piece]
+        all_posted(wf.at[k, 0:992, 0:width], gr_s.at[n])
+        if k != E:
+            all_posted(total_rows.at[k, :, 0:width], gr_s.at[6 + n])
 
     def terms_across(piece, lhs, rhs):
         _, k, first, width = pieces[piece]
@@ -504,18 +510,18 @@
     gather0(W)
     advance(1)
     gather3(E, (2, 3))
+    advance(2)
     gather2(U)
-    advance(2)
     gather1(W)
+    gather3(U, (0, 1))
     advance(3)
-    gather3(U, (0, 1))
     gather4(E)
+    gather5(E)
+
+    patches_arrive(0, px, 128)
+    partial_sums(0, px.at[128:256], E)
     to_patches(ts)
     patches_go(1, ts, tg, 0)
-    gather5(E)
-
-    patches_arrive(0, px, 128)
-    partial_sums(0, px.at[128:256], E)
     gather3(U, (2, 3))
     gather2(W)
     gather3(W, (0, 1))
@@ -559,7 +565,6 @@
         dyred[:, half(s)] = dy
         spread(2, s, dyf, 0, dy.astype(BF16))
     state_pass(0)
-    state_pass(1)
     spread_arrive(2, dyf, 0)
     terms_across("W", dyf, act)
     terms_here("W", dyf, act)
@@ -568,43 +573,45 @@
         dhid[:, cols] = (with_cols(dyf[...], W, cols) * slope[:, cols]).astype(BF16)
 
     reduce1("W")
+    state_pass(1)
     tiles(256, hidden_back)
     partial_sums(3, dhid, U)
-    state_pass(2)
-    state_pass(3)
     terms_across("U", nf, dhid)
     terms_here("U", nf, dhid)
     reduce1("U")
+    state_pass(2)
     reduce2("W")
     dn = all_summed(3)
     e = ered[...]
     recip = lax.rsqrt(jnp.mean(e * e, axis=1, keepdims=True) + 1e-06)
     de = dyred[...] + recip * dn - e * (recip * recip * recip) * jnp.mean(dn * e, axis=1, keepdims=True)
     spread_all(3, yd, 128, de.astype(BF16))
+    state_pass(3)
     reduce3("W")
     reduce2("U")
     spread_arrive(3, yd, 128)
-    terms_across("E0", yd, px)
-    terms_across("E1", yd, px)
+    for piece in parts:
+        terms_across(piece, yd, px)
     reduce4("W")
     reduce3("U")
-    terms_here("E0", yd, px)
-    terms_here("E1", yd, px)
-    reduce1("E0")
-    reduce1("E1")
+    for piece in parts:
+        terms_here(piece, yd, px)
+        reduce1(piece)
     reduce5("W")
     reduce4("U")
     reduce2("E0")
     reduce2("E1")
+    reduce2("E2")
     reduce5("U")
-    reduce3("E0")
-    reduce3("E1")
-    reduce4("E0")
-    reduce4("E1")
+    reduce2("E3")
+    for piece in parts:
+        reduce3(piece)
+    for piece in parts:
+        reduce4(piece)
     reduced("W")
     reduced("U")
-    reduce5("E0")
-    reduce5("E1")
+    for piece in parts:
+        reduce5(piece)
 
     for made in started:
         made.wait_send()
@@ -613,6 +620,7 @@
     all_posted(sbuf.at[0:3], rs_s.at[0])
     all_posted(sbuf.at[0:3], mg_s.at[0])
     for piece in pieces:
+        r_posted(piece)
         result(piece).wait()
 
     @pl.when(role == 1)
@@ -675,16 +683,16 @@
             pltpu.VMEM((3, 2, OWN, COLS), BF16),
             pltpu.VMEM((3, OWN, COLS), BF16),
             pltpu.VMEM((3, OWN, COLS), BF16),
-            dma((9,)), dma((4,)), dma((4,)), dma((8,)), dma((8,)),
+            dma((11,)), dma((4,)), dma((4,)), dma((8,)), dma((8,)),
             dma((3,)), dma((3,)),
             dma((2,)), dma((2,)),
             dma((3,)), dma((3, 13)),
             dma((1,)), dma((4, 2)),
             dma((1,)), dma((4,)),
-            dma((4, 8)), dma((4, 8)),
+            dma((8,)), dma((6, 8)),
         ],
         compiler_params=pltpu.CompilerParams(
-            collective_id=0, has_side_effects=True, vmem_limit_bytes=52 * 1024 * 1024
+            collective_id=0, has_side_effects=True, vmem_limit_bytes=60 * 1024 * 1024
         ),
         cost_estimate=pl.CostEstimate(flops=6 * 10**9, bytes_accessed=4 * 10**8, transcendentals=10**5),
     )(state, embed, mlp)

time: 114 us -> 111 us (0.974)
  local copies, waits for them, and re-layouts: 3.89 us -> 1.18 us
  Pallas kernels: 108 us -> 106 us
    unnamed x11 -> x13, local copies, waits for them, and re-layouts: 3.89 us -> 1.18 us
    pallas_call x1, Pallas kernels: 108 us -> 106 us  [train(): pl.pallas_call(kernel, name='train', out_shape=(jax.ShapeDtypeStruct((3,...]
where the time goes in v5:
time: 111 us; the launch traced here: 110 us
  Pallas kernels  106 us (95%)
  other arithmetic  2.46 us (2%)
  local copies, waits for them, and re-layouts  1.18 us (1%)
    pallas_call x1, Pallas kernels, train(): pl.pallas_call(kernel, name='train', out_shape=(jax.ShapeDtypeStruct((3,...  106 us

profile of v5, /device:TPU:8, one launch (start us, length us, event | category | flops | bytes accessed | tf_op | source)
XLA Modules:
  0.0 109.9 jit_solution(9060677004454162544)
XLA Ops:
  0.6 0.0 copy-start.5
  0.6 0.0 copy-start.3
  0.7 0.0 copy-start.2
  0.7 105.5 %train.1 = (f32[3,32,1024]{2,1,0:T(8,128)}, f32[2,8,64,128]{3,2,1,0:T(8,128)}) custom-call(f32[1,2,8,64,128]{4,3,2,1,0:T(8,128)} %state.1, bf16[1,32,1024]{2,1,0:T(8,128)(2,1)} %embed.1, bf16[1,2,32,1024]{3,2,1,0:T(8,128)(2,1)} %mlp.1), custom_call_target="tpu_custom_call" | custom-call | flops 6000000000 | bytes 400000000 | tf_op jit(solution)/shard_map/train/pallas_call | solution.py:644
  106.2 0.0 copy-start.1
  106.2 0.0 copy-done.5
  106.2 0.0 copy-done.3
  106.2 0.0 copy-start.4
  106.2 1.7 %subtract_convert_fusion.1 = (bf16[1,32,1024]{2,1,0:T(8,128)(2,1)}, f32[1,32,1024]{2,1,0:T(8,128)}) fusion(bf16[1,32,1024]{2,1,0:T(8,128)(2,1)S(1)} %copy-done.5, f32[3,32,1024]{2,1,0:T(8,128)} %get-tuple-element.8, f32[1,32,1024]{2,1,0:T(8,128)S(1)} %copy-done.3), kind=kLoop, calls=%fused_computation.2 | loop fusion | flops 196608 | bytes 524288 | tf_op jit(solution)/shard_map/convert_element_type | solution.py:705
  107.9 0.0 copy-done.2
  107.9 0.0 copy-done.1
  107.9 0.0 copy-done.4
  107.9 0.0 copy-start
  107.9 0.8 subtract_convert_fusion
  108.7 0.4 copy-done
  109.1 0.8 copy.11
Async XLA Ops:
  0.6 105.6 %copy-start.5 = (bf16[1,32,1024]{2,1,0:T(8,128)(2,1)S(1)}, bf16[1,32,1024]{2,1,0:T(8,128)(2,1)}, u32[]{:S(2)}) copy-start(bf16[1,32,1024]{2,1,0:T(8,128)(2,1)} %embed.1) | copy-start | bytes 196612
  0.6 105.6 %copy-start.3 = (f32[1,32,1024]{2,1,0:T(8,128)S(1)}, f32[1,32,1024]{2,1,0:T(8,128)}, u32[]{:S(2)}) copy-start(f32[1,32,1024]{2,1,0:T(8,128)} %param.8) | copy-start | bytes 393220
  0.7 107.2 %copy-start.2 = (f32[1,2,32,1024]{3,2,1,0:T(8,128)S(1)}, f32[1,2,32,1024]{3,2,1,0:T(8,128)}, u32[]{:S(2)}) copy-start(f32[1,2,32,1024]{3,2,1,0:T(8,128)} %param.9) | copy-start | bytes 786436
  106.2 1.7 %copy-start.1 = (f32[3,32,1024]{2,1,0:T(8,128)S(1)}, f32[3,32,1024]{2,1,0:T(8,128)}, u32[]{:S(2)}) copy-start(f32[3,32,1024]{2,1,0:T(8,128)} %get-tuple-element.8) | copy-start | bytes 1179652
  106.2 1.7 %copy-start.4 = (bf16[1,2,32,1024]{3,2,1,0:T(8,128)(2,1)S(1)}, bf16[1,2,32,1024]{3,2,1,0:T(8,128)(2,1)}, u32[]{:S(2)}) copy-start(bf16[1,2,32,1024]{3,2,1,0:T(8,128)(2,1)} %mlp.1) | copy-start | bytes 393220
  107.9 1.2 %copy-start = (f32[2,8,64,128]{3,2,1,0:T(8,128)S(1)}, f32[2,8,64,128]{3,2,1,0:T(8,128)}, u32[]{:S(2)}) copy-start(f32[2,8,64,128]{3,2,1,0:T(8,128)} %get-tuple-element.18) | copy-start | bytes 1572868

commit v6 on v5

--- a/solution.py
+++ b/solution.py
@@ -30,7 +30,7 @@
 
 def kernel(
     state, embed, mlp, out, state_out,
-    total_rows, field, passed, edge, edges, onehot, spread_in, xs, ts, wf, px, yd, tg, part, sbuf, rbuf, nf, dyf, act, slope, dhid, ered, dyred,
+    total_rows, field, final, passed, edge, edges, onehot, spread_in, xs, ts, wf, px, yd, tg, part, sbuf, rbuf, nf, dyf, act, slope, dhid, ered, dyred,
     acc, cs, cr, xs1, xr1, xs2, xr2, vsum, zs1, zr1, zs2, zr2,
     in_s, halo_s, halo_r, state_s, state_r, role_s, role_r, x_s, x_r, ag_s, ag_r, rs_s, rs_r, mg_s, mg_r, gr_s, gr_r,
 ):
@@ -126,26 +126,39 @@
     def state_part(whole, part):
         return whole.at[part // 2, pl.ds(4 * (part % 2), 4)]
 
-    def final_part(part):
-        return field.at[0, part // 2, pl.ds(4 * (part % 2), 4), pl.ds(8, 64), pl.ds(0, 128)]
-
     def state_across(part):
-        return copy(final_part(part), state_part(passed, part), state_s.at[part], state_r.at[part],
+        return copy(state_part(final, part), state_part(passed, part), state_s.at[part], state_r.at[part],
                     {"role": 1, "dp": mirror})
 
+    def state_home(part):
+        return copy(state_part(passed, part), state_part(final, part), state_s.at[4 + part], state_r.at[4 + part],
+                    {"dp": mirror})
+
     def state_here(part):
-        return pltpu.make_async_copy(final_part(part), state_part(state_out, part), in_s.at[1 + part])
-
-    def state_home(part):
-        return copy(state_part(passed, part), state_part(state_out, part), state_s.at[4 + part], state_r.at[4 + part],
-                    {"dp": mirror})
-
-    def state_go(first):
+        rounded = field.at[1, part // 2, pl.ds(4 * (part % 2), 4), pl.ds(8, 64), pl.ds(0, 128)]
+        return pltpu.make_async_copy(rounded, state_part(state_out, part), in_s.at[1 + part])
+
+    def state_widen(part):
+        species, planes = part // 2, pl.ds(4 * (part % 2), 4)
+        field[1, species, planes, 8:72, 0:128] = final[species, planes].astype(F32)
+        state_here(part).start()
+
+    def state_go():
         @pl.when(role == 0)
         def _():
-            for part in (first, first + 1):
+            for part in range(4):
+                species, planes = part // 2, pl.ds(4 * (part % 2), 4)
+                final[species, planes] = field[0, species, planes, 8:72, 0:128].astype(BF16)
                 state_across(part).start()
-                state_here(part).start()
+            for part in range(4):
+                state_widen(part)
+
+    def state_arrive():
+        @pl.when(role == 1)
+        def _():
+            for part in range(4):
+                state_home(part).wait_recv()
+                state_widen(part)
 
     def state_pass(part):
         @pl.when(role == 1)
@@ -547,7 +560,7 @@
     gather4(W)
     gather5(W)
     partial_sums(1, act, W)
-    state_go(0)
+    state_go()
     for s in (0, 1):
         spread(1, s, yd, 0, (ered[:, half(s)] + summed(1, s)).astype(BF16))
     patches_arrive(1, tg, 0)
@@ -559,12 +572,12 @@
 
     tiles(256, residual)
     partial_sums(2, px.at[0:128], E)
-    state_go(2)
     for s in (0, 1):
         dy = summed(2, s)
         dyred[:, half(s)] = dy
         spread(2, s, dyf, 0, dy.astype(BF16))
     state_pass(0)
+    state_pass(1)
     spread_arrive(2, dyf, 0)
     terms_across("W", dyf, act)
     terms_here("W", dyf, act)
@@ -573,20 +586,19 @@
         dhid[:, cols] = (with_cols(dyf[...], W, cols) * slope[:, cols]).astype(BF16)
 
     reduce1("W")
-    state_pass(1)
+    state_pass(2)
+    state_pass(3)
     tiles(256, hidden_back)
     partial_sums(3, dhid, U)
     terms_across("U", nf, dhid)
     terms_here("U", nf, dhid)
     reduce1("U")
-    state_pass(2)
     reduce2("W")
     dn = all_summed(3)
     e = ered[...]
     recip = lax.rsqrt(jnp.mean(e * e, axis=1, keepdims=True) + 1e-06)
     de = dyred[...] + recip * dn - e * (recip * recip * recip) * jnp.mean(dn * e, axis=1, keepdims=True)
     spread_all(3, yd, 128, de.astype(BF16))
-    state_pass(3)
     reduce3("W")
     reduce2("U")
     spread_arrive(3, yd, 128)
@@ -604,6 +616,7 @@
     reduce2("E2")
     reduce5("U")
     reduce2("E3")
+    state_arrive()
     for piece in parts:
         reduce3(piece)
     for piece in parts:
@@ -619,6 +632,8 @@
         all_posted(wf.at[k, 0:992], ag_s.at[k])
     all_posted(sbuf.at[0:3], rs_s.at[0])
     all_posted(sbuf.at[0:3], mg_s.at[0])
+    for part in range(4):
+        state_here(part).wait()
     for piece in pieces:
         r_posted(piece)
         result(piece).wait()
@@ -628,7 +643,7 @@
         for k in (E, U, W):
             weights_across(k).wait_send()
         for part in range(4):
-            state_home(part).wait()
+            state_home(part).wait_send()
 
     @pl.when(role == 0)
     def _():
@@ -636,7 +651,6 @@
             all_posted(px.at[0:224], x_s.at[which])
         for part in range(4):
             state_across(part).wait_send()
-            state_here(part).wait()
 
 
 def train(state, embed, mlp):
@@ -650,7 +664,8 @@
         scratch_shapes=[
             pltpu.VMEM((3, OWN, COLS), F32),
             pltpu.VMEM((2, 2, 8, 80, 256), F32),
-            pltpu.VMEM((2, 8, 64, 128), F32),
+            pltpu.VMEM((2, 8, 64, 128), BF16),
+            pltpu.VMEM((2, 8, 64, 128), BF16),
             pltpu.VMEM((2, 80, 128), F32),
             pltpu.VMEM((2, 80, 128), F32),
             pltpu.VMEM((2048, 256), BF16),

time: 111 us -> 111 us (level)
  no operation moved by 1% of the time
where the time goes in v6:
time: 111 us; the launch traced here: 109 us
  Pallas kernels  105 us (95%)
  other arithmetic  2.46 us (2%)
  local copies, waits for them, and re-layouts  1.18 us (1%)
    pallas_call x1, Pallas kernels, train(): pl.pallas_call(kernel, name='train', out_shape=(jax.ShapeDtypeStruct((3,...  105 us

profile of v6, /device:TPU:8, one launch (start us, length us, event | category | flops | bytes accessed | tf_op | source)
XLA Modules:
  0.0 109.5 jit_solution(4083350852766581888)
XLA Ops:
  0.6 0.0 copy-start.5
  0.6 0.0 copy-start.3
  0.7 0.0 copy-start.2
  0.7 105.1 %train.1 = (f32[3,32,1024]{2,1,0:T(8,128)}, f32[2,8,64,128]{3,2,1,0:T(8,128)}) custom-call(f32[1,2,8,64,128]{4,3,2,1,0:T(8,128)} %state.1, bf16[1,32,1024]{2,1,0:T(8,128)(2,1)} %embed.1, bf16[1,2,32,1024]{3,2,1,0:T(8,128)(2,1)} %mlp.1), custom_call_target="tpu_custom_call" | custom-call | flops 6000000000 | bytes 400000000 | tf_op jit(solution)/shard_map/train/pallas_call | solution.py:658
  105.8 0.0 copy-start.1
  105.8 0.0 copy-done.5
  105.8 0.0 copy-done.3
  105.8 0.0 copy-start.4
  105.8 1.7 %subtract_convert_fusion.1 = (bf16[1,32,1024]{2,1,0:T(8,128)(2,1)}, f32[1,32,1024]{2,1,0:T(8,128)}) fusion(bf16[1,32,1024]{2,1,0:T(8,128)(2,1)S(1)} %copy-done.5, f32[3,32,1024]{2,1,0:T(8,128)} %get-tuple-element.8, f32[1,32,1024]{2,1,0:T(8,128)S(1)} %copy-done.3), kind=kLoop, calls=%fused_computation.2 | loop fusion | flops 196608 | bytes 524288 | tf_op jit(solution)/shard_map/convert_element_type | solution.py:720
  107.5 0.0 copy-done.2
  107.5 0.0 copy-done.1
  107.5 0.0 copy-done.4
  107.5 0.0 copy-start
  107.5 0.8 subtract_convert_fusion
  108.3 0.4 copy-done
  108.7 0.8 copy.11
Async XLA Ops:
  0.6 105.2 %copy-start.5 = (bf16[1,32,1024]{2,1,0:T(8,128)(2,1)S(1)}, bf16[1,32,1024]{2,1,0:T(8,128)(2,1)}, u32[]{:S(2)}) copy-start(bf16[1,32,1024]{2,1,0:T(8,128)(2,1)} %embed.1) | copy-start | bytes 196612
  0.6 105.2 %copy-start.3 = (f32[1,32,1024]{2,1,0:T(8,128)S(1)}, f32[1,32,1024]{2,1,0:T(8,128)}, u32[]{:S(2)}) copy-start(f32[1,32,1024]{2,1,0:T(8,128)} %param.8) | copy-start | bytes 393220
  0.7 106.8 %copy-start.2 = (f32[1,2,32,1024]{3,2,1,0:T(8,128)S(1)}, f32[1,2,32,1024]{3,2,1,0:T(8,128)}, u32[]{:S(2)}) copy-start(f32[1,2,32,1024]{3,2,1,0:T(8,128)} %param.9) | copy-start | bytes 786436
  105.8 1.7 %copy-start.1 = (f32[3,32,1024]{2,1,0:T(8,128)S(1)}, f32[3,32,1024]{2,1,0:T(8,128)}, u32[]{:S(2)}) copy-start(f32[3,32,1024]{2,1,0:T(8,128)} %get-tuple-element.8) | copy-start | bytes 1179652
  105.8 1.7 %copy-start.4 = (bf16[1,2,32,1024]{3,2,1,0:T(8,128)(2,1)S(1)}, bf16[1,2,32,1024]{3,2,1,0:T(8,128)(2,1)}, u32[]{:S(2)}) copy-start(bf16[1,2,32,1024]{3,2,1,0:T(8,128)(2,1)} %mlp.1) | copy-start | bytes 393220
  107.5 1.2 %copy-start = (f32[2,8,64,128]{3,2,1,0:T(8,128)S(1)}, f32[2,8,64,128]{3,2,1,0:T(8,128)}, u32[]{:S(2)}) copy-start(f32[2,8,64,128]{3,2,1,0:T(8,128)} %get-tuple-element.18) | copy-start | bytes 1572868

commit v7 on v6

--- a/solution.py
+++ b/solution.py
@@ -314,8 +314,8 @@
     def gather5(k):
         g_arrive(k, 12, c1 * 512, 512, to_c)
 
-    def tiles(width, body):
-        @pl.loop(0, COLS // width)
+    def tiles(width, body, first=0, last=COLS):
+        @pl.loop(first // width, last // width)
         def _(t):
             body(pl.ds(pl.multiple_of(t * width, width), width))
 
@@ -556,8 +556,9 @@
             1.0 + 3.0 * 0.044715 * square
         )
 
-    tiles(256, hidden)
+    tiles(256, hidden, 0, 512)
     gather4(W)
+    tiles(256, hidden, 512, 1024)
     gather5(W)
     partial_sums(1, act, W)
     state_go()

time: 111 us -> 112 us (level)
  no operation moved by 1% of the time
where the time goes in v7:
time: 112 us; the launch traced here: 110 us
  Pallas kernels  106 us (95%)
  other arithmetic  2.46 us (2%)
  local copies, waits for them, and re-layouts  1.18 us (1%)
    pallas_call x1, Pallas kernels, train(): pl.pallas_call(kernel, name='train', out_shape=(jax.ShapeDtypeStruct((3,...  106 us

profile of v7, /device:TPU:8, one launch (start us, length us, event | category | flops | bytes accessed | tf_op | source)
XLA Modules:
  0.0 110.2 jit_solution(16384147783718154872)
XLA Ops:
  0.6 0.0 copy-start.5
  0.6 0.0 copy-start.3
  0.7 0.0 copy-start.2
  0.7 105.8 %train.1 = (f32[3,32,1024]{2,1,0:T(8,128)}, f32[2,8,64,128]{3,2,1,0:T(8,128)}) custom-call(f32[1,2,8,64,128]{4,3,2,1,0:T(8,128)} %state.1, bf16[1,32,1024]{2,1,0:T(8,128)(2,1)} %embed.1, bf16[1,2,32,1024]{3,2,1,0:T(8,128)(2,1)} %mlp.1), custom_call_target="tpu_custom_call" | custom-call | flops 6000000000 | bytes 400000000 | tf_op jit(solution)/shard_map/train/pallas_call | solution.py:659
  106.5 0.0 copy-start.1
  106.5 0.0 copy-done.5
  106.5 0.0 copy-done.3
  106.5 0.0 copy-start.4
  106.5 1.7 %subtract_convert_fusion.1 = (bf16[1,32,1024]{2,1,0:T(8,128)(2,1)}, f32[1,32,1024]{2,1,0:T(8,128)}) fusion(bf16[1,32,1024]{2,1,0:T(8,128)(2,1)S(1)} %copy-done.5, f32[3,32,1024]{2,1,0:T(8,128)} %get-tuple-element.8, f32[1,32,1024]{2,1,0:T(8,128)S(1)} %copy-done.3), kind=kLoop, calls=%fused_computation.2 | loop fusion | flops 196608 | bytes 524288 | tf_op jit(solution)/shard_map/convert_element_type | solution.py:721
  108.2 0.0 copy-done.2
  108.2 0.0 copy-done.1
  108.2 0.0 copy-done.4
  108.2 0.0 copy-start
  108.2 0.8 subtract_convert_fusion
  109.0 0.4 copy-done
  109.4 0.8 copy.11
Async XLA Ops:
  0.6 105.9 %copy-start.5 = (bf16[1,32,1024]{2,1,0:T(8,128)(2,1)S(1)}, bf16[1,32,1024]{2,1,0:T(8,128)(2,1)}, u32[]{:S(2)}) copy-start(bf16[1,32,1024]{2,1,0:T(8,128)(2,1)} %embed.1) | copy-start | bytes 196612
  0.6 105.9 %copy-start.3 = (f32[1,32,1024]{2,1,0:T(8,128)S(1)}, f32[1,32,1024]{2,1,0:T(8,128)}, u32[]{:S(2)}) copy-start(f32[1,32,1024]{2,1,0:T(8,128)} %param.8) | copy-start | bytes 393220
  0.7 107.5 %copy-start.2 = (f32[1,2,32,1024]{3,2,1,0:T(8,128)S(1)}, f32[1,2,32,1024]{3,2,1,0:T(8,128)}, u32[]{:S(2)}) copy-start(f32[1,2,32,1024]{3,2,1,0:T(8,128)} %param.9) | copy-start | bytes 786436
  106.5 1.7 %copy-start.1 = (f32[3,32,1024]{2,1,0:T(8,128)S(1)}, f32[3,32,1024]{2,1,0:T(8,128)}, u32[]{:S(2)}) copy-start(f32[3,32,1024]{2,1,0:T(8,128)} %get-tuple-element.8) | copy-start | bytes 1179652
  106.5 1.7 %copy-start.4 = (bf16[1,2,32,1024]{3,2,1,0:T(8,128)(2,1)S(1)}, bf16[1,2,32,1024]{3,2,1,0:T(8,128)(2,1)}, u32[]{:S(2)}) copy-start(bf16[1,2,32,1024]{3,2,1,0:T(8,128)(2,1)} %mlp.1) | copy-start | bytes 393220
  108.2 1.2 %copy-start = (f32[2,8,64,128]{3,2,1,0:T(8,128)S(1)}, f32[2,8,64,128]{3,2,1,0:T(8,128)}, u32[]{:S(2)}) copy-start(f32[2,8,64,128]{3,2,1,0:T(8,128)} %get-tuple-element.18) | copy-start | bytes 1572868
